TPU v7x, 32 devices: a whole 2x2x4 slice. The times are simulated.
32 devices in a mesh: grp: 2 (over y), row: 8 (over z, x), sub: 2 (over core).
Axes of the slice: x: 2, y: 2, z: 4, core: 2. Of those that a mesh axis runs over, the one named last changes fastest.
Arguments:
- right_sides: bfloat16 [32768, 256], P(('grp', 'row', 'sub')), parts along dimension 0, may hold values from -6 to 6
- leaf_inverse: bfloat16 [32768, 512], P(('grp', 'row', 'sub')), parts along dimension 0, may hold values from -0.25 to 0.25
- basis_one: bfloat16 [32768, 256], P(('grp', 'row', 'sub')), parts along dimension 0, may hold values from -1.5 to 1.5
- basis_two: bfloat16 [32768, 256], P(('grp', 'row', 'sub')), parts along dimension 0, may hold values from -1.5 to 1.5
- basis_three: bfloat16 [32768, 256], P(('grp', 'row', 'sub')), parts along dimension 0, may hold values from -1.5 to 1.5
- capacity_one: bfloat16 [1024, 512], P('grp'), parts along dimension 0, may hold values from -0.01171875 to 0.01171875
- capacity_two: bfloat16 [1024, 512], P('grp'), parts along dimension 0, may hold values from -0.005859375 to 0.005859375
- capacity_three: bfloat16 [1024, 512], P('grp'), parts along dimension 0, may hold values from -0.0029296875 to 0.0029296875
Outputs:
- solution: bfloat16 [32768, 256], P(('grp', 'row', 'sub')), parts along dimension 0
There are 2 independent parts, one for each index of `grp`. A program takes and returns all parts, laid end to end along the dimension named above; each array names one. Nothing has to cross between parts.
All inputs are finite; a program needn't handle non-finite values.
Results may differ from a plain program's by a relative error of at most 0.008.
Values sent between devices are 32-bit elements; how exact they have to be, the bound alone decides.
No kernel may reach another device: no remote copies, remote signals or barrier semaphores. Data moves between devices by JAX's collectives and lax.ppermute only.
A program may use at most 64 MiB of HBM per device.

v0:
```python
import jax
import jax.numpy as jnp
from jax import lax
from jax.sharding import PartitionSpec as P


def from_partner(array, axis, stride):
    return lax.ppermute(array, axis, [(i, i ^ 1 << stride) for i in range(lax.axis_size(axis))])


def project(basis, field):
    return jnp.einsum(
        "rk,rm->km", basis, field.astype(jnp.bfloat16), preferred_element_type=jnp.float32
    )


def core_total(projected):
    return lax.psum(projected, "sub")


def pair_sum(projected, low_bits):
    for bit_index in range(low_bits):
        projected = projected + from_partner(projected, "row", bit_index)
    sibling_sum = from_partner(projected, "row", low_bits)
    return (projected, sibling_sum)


def pair_stack(own_sum, sibling_sum, child_side):
    first = jnp.where(child_side == 0, own_sum, sibling_sum)
    second = jnp.where(child_side == 0, sibling_sum, own_sum)
    return jnp.concatenate([first, second], axis=0)


def correct(field, basis, capacity, stacked, child_side):
    basis_rank = basis.shape[1]
    own_rows = lax.dynamic_slice_in_dim(capacity, child_side * basis_rank, basis_rank, 0)
    coefficients = jnp.dot(
        own_rows.astype(jnp.float32),
        stacked,
        precision=lax.Precision.HIGHEST,
        preferred_element_type=jnp.float32,
    )
    return field - jnp.dot(
        basis, coefficients.astype(jnp.bfloat16), preferred_element_type=jnp.float32
    )


def per_device(
    right_sides,
    leaf_inverse,
    basis_one,
    basis_two,
    basis_three,
    capacity_one,
    capacity_two,
    capacity_three,
):
    leaf_order = leaf_inverse.shape[1]
    leaves = leaf_inverse.shape[0] // leaf_order
    width_rhs = right_sides.shape[1]
    basis_rank = basis_one.shape[1]
    field = jnp.einsum(
        "lij,ljm->lim",
        leaf_inverse.reshape(leaves, leaf_order, leaf_order),
        right_sides.reshape(leaves, leaf_order, width_rhs),
        preferred_element_type=jnp.float32,
    )
    field = field.reshape(leaves * leaf_order, width_rhs)
    nodes = leaves // 2
    blocks = basis_one.reshape(nodes, 2, leaf_order, basis_rank)
    rounded = field.astype(jnp.bfloat16).reshape(nodes, 2, leaf_order, width_rhs)
    projection = jnp.einsum(
        "ncrk,ncrm->nckm", blocks, rounded, preferred_element_type=jnp.float32
    ).reshape(nodes, 2 * basis_rank, width_rhs)
    coefficients = jnp.einsum(
        "ij,njm->nim",
        capacity_one.astype(jnp.float32),
        projection,
        precision=lax.Precision.HIGHEST,
        preferred_element_type=jnp.float32,
    )
    coefficients = coefficients.astype(jnp.bfloat16).reshape(nodes, 2, basis_rank, width_rhs)
    update = jnp.einsum("ncrk,nckm->ncrm", blocks, coefficients, preferred_element_type=jnp.float32)
    field = field - update.reshape(leaves * leaf_order, width_rhs)
    row_count = lax.axis_size("row")
    row_index = lax.axis_index("row")
    width_two = row_count // 8
    width_three = row_count // 2
    side_two = row_index // width_two % 2
    side_three = row_index // width_three % 2
    own_sum, sibling_sum = pair_sum(
        core_total(project(basis_two, field)), width_two.bit_length() - 1
    )
    field = correct(
        field, basis_two, capacity_two, pair_stack(own_sum, sibling_sum, side_two), side_two
    )
    own_sum, sibling_sum = pair_sum(
        core_total(project(basis_three, field)), width_three.bit_length() - 1
    )
    field = correct(
        field, basis_three, capacity_three, pair_stack(own_sum, sibling_sum, side_three), side_three
    )
    return field.astype(jnp.bfloat16)


def solution(mesh):
    in_specs = (
        P(("grp", "row", "sub"), None),
        P(("grp", "row", "sub"), None),
        P(("grp", "row", "sub"), None),
        P(("grp", "row", "sub"), None),
        P(("grp", "row", "sub"), None),
        P("grp", None),
        P("grp", None),
        P("grp", None),
    )
    out_specs = P(("grp", "row", "sub"), None)
    return jax.shard_map(
        per_device, mesh=mesh, in_specs=in_specs, out_specs=out_specs, check_vma=False
    )
```

profile of v0, /device:TPU:0, one launch (start us, length us, event | category | flops | bytes accessed | tf_op | source)
XLA Modules:
  0.0 107.7 jit_solution(3195078000139913431)
XLA Ops:
  6.5 1.2 %copy-done = bf16[1024,512]{1,0:T(8,128)(2,1)S(1)} copy-done((bf16[1024,512]{1,0:T(8,128)(2,1)S(1)}, bf16[1024,512]{1,0:T(8,128)(2,1)}, u32[]{:S(2)}) %copy-start) | copy-done | bytes 1048600
  7.8 1.5 %fusion.22 = f32[2,512,256]{2,1,0:T(8,128)S(1)} fusion(bf16[2,512,512]{2,1,0:T(8,128)(2,1)S(1)} %bitcast.43, bf16[2,512,256]{2,1,0:T(8,128)(2,1)} %bitcast.49), kind=kOutput, calls=%fused_computation.34 | convolution fusion | flops 268435456 | bytes 2621440 | tf_op jit(solution)/shard_map/lij,ljm->lim/dot_general | solution.py:62
  9.7 0.7 copy-done.6
  10.4 1.0 fusion.4
  11.5 1.4 %fusion.2 = f32[2,512,256]{2,1,0:T(8,128)S(1)} fusion(f32[2,512,256]{2,1,0:T(8,128)S(1)} %fusion.22, bf16[2,512,256]{2,1,0:T(8,128)(2,1)} %bitcast.47, bf16[2,256,256]{1,0,2:T(2,128)(2,1)S(1)} %reshape.41), kind=kOutput, calls=%fused_computation.5 | convolution fusion | flops 134479872 | bytes 2883584 | tf_op jit(solution)/shard_map/ncrk,nckm->ncrm/dot_general | solution.py:83
  12.9 1.0 convolution_bitcast_fusion.4
  14.1 21.1 %all-reduce.3.cloned.1.call-done = f32[256,256]{0,1:T(8,128)} async-done(((f32[256,256]{0,1:T(8,128)}), f32[256,256]{0,1:T(8,128)}) %all-reduce.3.cloned.1.call-update) | async-done | bytes 262160 | tf_op jit(solution)/shard_map/psum | solution.py:18
  35.1 1.8 %collective-permute-start = (f32[256,256]{0,1:T(8,128)}, f32[256,256]{0,1:T(8,128)}, u32[]{:S(2)}, u32[]{:S(2)}) collective-permute-start(f32[256,256]{0,1:T(8,128)} %all-reduce.3.cloned.1.call-done), channel_id=1, source_target_pairs={{0,2},{2,0},{4,6},{6,4},{8,10},{10,8},{12,14},{14,12},{1,3},{3,1},... | collective-permute-start | bytes 786440 | tf_op jit(solution)/shard_map/ppermute | solution.py:8
  37.3 6.7 %collective-permute-done = f32[256,256]{0,1:T(8,128)} collective-permute-done((f32[256,256]{0,1:T(8,128)}, f32[256,256]{0,1:T(8,128)}, u32[]{:S(2)}, u32[]{:S(2)}) %collective-permute-start) | collective-permute-done | bytes 262176 | tf_op jit(solution)/shard_map/ppermute | solution.py:8
  43.9 1.0 broadcast_select_fusion.3
  45.4 0.6 copy-done.4
  46.3 0.7 copy-done.1
  47.0 1.0 convolution_bitcast_fusion.3
  48.0 19.6 %all-reduce.5.cloned.1.call-done = f32[256,256]{0,1:T(8,128)} async-done(((f32[256,256]{0,1:T(8,128)}), f32[256,256]{0,1:T(8,128)}) %all-reduce.5.cloned.1.call-update) | async-done | bytes 262160 | tf_op jit(solution)/shard_map/psum | solution.py:18
  67.6 1.8 %collective-permute-start.1 = (f32[256,256]{0,1:T(8,128)}, f32[256,256]{0,1:T(8,128)S(1)}, u32[]{:S(2)}, u32[]{:S(2)}) collective-permute-start(f32[256,256]{0,1:T(8,128)} %all-reduce.5.cloned.1.call-done), channel_id=1, source_target_pairs={{0,2},{2,0},{4,6},{6,4},{8,10},{10,8},{12,14},{14,12},{1,3},{3,1},... | collective-permute-start | bytes 786440 | tf_op jit(solution)/shard_map/ppermute | solution.py:8
  69.4 6.9 %collective-permute-done.1 = f32[256,256]{0,1:T(8,128)S(1)} collective-permute-done((f32[256,256]{0,1:T(8,128)}, f32[256,256]{0,1:T(8,128)S(1)}, u32[]{:S(2)}, u32[]{:S(2)}) %collective-permute-start.1) | collective-permute-done | bytes 262176 | tf_op jit(solution)/shard_map/ppermute | solution.py:8
  76.3 1.0 add.29
  77.3 1.8 %collective-permute-start.2 = (f32[256,256]{0,1:T(8,128)S(1)}, f32[256,256]{0,1:T(8,128)S(1)}, u32[]{:S(2)}, u32[]{:S(2)}) collective-permute-start(f32[256,256]{0,1:T(8,128)S(1)} %add.29), channel_id=1, source_target_pairs={{0,4},{2,6},{4,0},{6,2},{8,12},{10,14},{12,8},{14,10},{1,5},{3,7},... | collective-permute-start | bytes 786440 | tf_op jit(solution)/shard_map/ppermute | solution.py:8
  79.1 5.9 %collective-permute-done.2 = f32[256,256]{0,1:T(8,128)S(1)} collective-permute-done((f32[256,256]{0,1:T(8,128)S(1)}, f32[256,256]{0,1:T(8,128)S(1)}, u32[]{:S(2)}, u32[]{:S(2)}) %collective-permute-start.2) | collective-permute-done | bytes 262176 | tf_op jit(solution)/shard_map/ppermute | solution.py:8
  85.0 2.7 %collective-permute-start.3 = (f32[256,256]{0,1:T(8,128)S(1)}, f32[256,256]{0,1:T(8,128)S(1)}, u32[]{:S(2)}, u32[]{:S(2)}) collective-permute-start(f32[256,256]{0,1:T(8,128)S(1)} %add.30), channel_id=1, source_target_pairs={{0,8},{2,10},{4,12},{6,14},{8,0},{10,2},{12,4},{14,6},{1,9},{3,11}... | collective-permute-start | bytes 786440 | tf_op jit(solution)/shard_map/ppermute | solution.py:8
  87.7 10.6 %collective-permute-done.3 = f32[256,256]{0,1:T(8,128)S(1)} collective-permute-done((f32[256,256]{0,1:T(8,128)S(1)}, f32[256,256]{0,1:T(8,128)S(1)}, u32[]{:S(2)}, u32[]{:S(2)}) %collective-permute-start.3) | collective-permute-done | bytes 262176 | tf_op jit(solution)/shard_map/ppermute | solution.py:8
  98.5 0.4 convolution_convert_fusion.1
  98.9 0.6 copy-done.2
  99.8 1.0 copy.13
  (27 shorter events, 2.1 us)
Async XLA Ops:
  6.5 1.2 %copy-start = (bf16[1024,512]{1,0:T(8,128)(2,1)S(1)}, bf16[1024,512]{1,0:T(8,128)(2,1)}, u32[]{:S(2)}) copy-start(bf16[1024,512]{1,0:T(8,128)(2,1)} %param.9) | copy-start | bytes 3145732
  6.5 28.6 %all-reduce.3.cloned.1.call-start = ((), (), s32[]{:S(2)}) async-start(), calls=%async_computation | async-start | bytes 524288 | tf_op jit(solution)/shard_map/psum | solution.py:18
  7.8 1.5 %copy-start.5 = (bf16[1024,256]{1,0:T(8,128)(2,1)S(1)}, bf16[1024,256]{1,0:T(8,128)(2,1)}, u32[]{:S(2)}) copy-start(bf16[1024,256]{1,0:T(8,128)(2,1)} %param.10) | copy-start | bytes 1572868
  9.3 1.0 copy-start.6
  11.5 1.4 %copy-start.3 = (bf16[1024,256]{1,0:T(8,128)(2,1)S(1)}, bf16[1024,256]{1,0:T(8,128)(2,1)}, u32[]{:S(2)}) copy-start(bf16[1024,256]{1,0:T(8,128)(2,1)} %param.11) | copy-start | bytes 1572868
  14.0 53.6 %all-reduce.5.cloned.1.call-start = ((), (), s32[]{:S(2)}) async-start(), calls=%async_computation.1 | async-start | bytes 524288 | tf_op jit(solution)/shard_map/psum | solution.py:18
  35.1 8.8 %collective-permute-start = (f32[256,256]{0,1:T(8,128)}, f32[256,256]{0,1:T(8,128)}, u32[]{:S(2)}, u32[]{:S(2)}) collective-permute-start(f32[256,256]{0,1:T(8,128)} %all-reduce.3.cloned.1.call-done), channel_id=1, source_target_pairs={{0,2},{2,0},{4,6},{6,4},{8,10},{10,8},{12,14},{14,12},{1,3},{3,1},... | collective-permute-start | bytes 786440 | tf_op jit(solution)/shard_map/ppermute | solution.py:8
  36.9 7.0 %copy-start.7 = (f32[256,256]{0,1:T(8,128)S(1)}, f32[256,256]{0,1:T(8,128)}, u32[]{:S(2)}) copy-start(f32[256,256]{0,1:T(8,128)} %all-reduce.3.cloned.1.call-done) | copy-start | bytes 786436
  37.2 7.7 %copy-start.8 = (bf16[512,512]{1,0:T(8,128)(2,1)S(1)}, bf16[512,512]{1,0:T(8,128)(2,1)}, u32[]{:S(2)}) copy-start(bf16[512,512]{1,0:T(8,128)(2,1)} %param.14) | copy-start | bytes 1572868
  44.9 1.0 copy-start.4
  46.0 1.0 copy-start.1
  67.6 8.7 %collective-permute-start.1 = (f32[256,256]{0,1:T(8,128)}, f32[256,256]{0,1:T(8,128)S(1)}, u32[]{:S(2)}, u32[]{:S(2)}) collective-permute-start(f32[256,256]{0,1:T(8,128)} %all-reduce.5.cloned.1.call-done), channel_id=1, source_target_pairs={{0,2},{2,0},{4,6},{6,4},{8,10},{10,8},{12,14},{14,12},{1,3},{3,1},... | collective-permute-start | bytes 786440 | tf_op jit(solution)/shard_map/ppermute | solution.py:8
  77.3 7.7 %collective-permute-start.2 = (f32[256,256]{0,1:T(8,128)S(1)}, f32[256,256]{0,1:T(8,128)S(1)}, u32[]{:S(2)}, u32[]{:S(2)}) collective-permute-start(f32[256,256]{0,1:T(8,128)S(1)} %add.29), channel_id=1, source_target_pairs={{0,4},{2,6},{4,0},{6,2},{8,12},{10,14},{12,8},{14,10},{1,5},{3,7},... | collective-permute-start | bytes 786440 | tf_op jit(solution)/shard_map/ppermute | solution.py:8
  85.0 13.4 %collective-permute-start.3 = (f32[256,256]{0,1:T(8,128)S(1)}, f32[256,256]{0,1:T(8,128)S(1)}, u32[]{:S(2)}, u32[]{:S(2)}) collective-permute-start(f32[256,256]{0,1:T(8,128)S(1)} %add.30), channel_id=1, source_target_pairs={{0,8},{2,10},{4,12},{6,14},{8,0},{10,2},{12,4},{14,6},{1,9},{3,11}... | collective-permute-start | bytes 786440 | tf_op jit(solution)/shard_map/ppermute | solution.py:8
  87.7 10.7 %copy-start.9 = (bf16[512,512]{1,0:T(8,128)(2,1)S(1)}, bf16[512,512]{1,0:T(8,128)(2,1)}, u32[]{:S(2)}) copy-start(bf16[512,512]{1,0:T(8,128)(2,1)} %param.15) | copy-start | bytes 1572868
  98.4 1.0 copy-start.2
Sparse Core Ops, SparseCore 0:
  14.1 20.9 all-reduce.2
  48.2 19.3 all-reduce.4
where the time goes:
time: 108 us
  waiting for transfers between devices  70.8 us (66%)
  between operations  13.6 us (13%)
  starting transfers between devices  8.13 us (8%)
  matrix products  7.98 us (7%)
  local copies, waits for them, and re-layouts  5.16 us (5%)
  other arithmetic  2.04 us (2%)
    psum x2, waiting for transfers between devices, core_total(): return lax.psum(projected, 'sub')  40.6 us
    ppermute x4, waiting for transfers between devices, from_partner(): lax.ppermute(array, axis, [(i, i ^ 1 << stride) for i in range(lax.axis_s...  30.1 us
    ppermute x4, starting transfers between devices, from_partner(): lax.ppermute(array, axis, [(i, i ^ 1 << stride) for i in range(lax.axis_s...  8.09 us
    unnamed x20, local copies, waits for them, and re-layouts  3.77 us
  transfers between devices with their start and end apart: 6, of which 6 were waited for; matrix products, arithmetic and copies ran while one was open for 0% of the time, Pallas kernels for 0%

commit v1 on v0

--- a/solution.py
+++ b/solution.py
@@ -15,7 +15,7 @@
 
 
 def core_total(projected):
-    return lax.psum(projected, "sub")
+    return projected + from_partner(projected, "sub", 0)
 
 
 def pair_sum(projected, low_bits):

time: 108 us -> 55.5 us (0.51)
  waiting for transfers between devices: 70.8 us -> 31.9 us
  between operations: 13.6 us -> 0.21 us
  starting transfers between devices: 8.13 us -> 10 us
  matrix products: 7.98 us -> 6.61 us
    psum x2 -> x0, waiting for transfers between devices: 40.6 us -> none  [core_total(): return lax.psum(projected, 'sub')]
    ppermute x4 -> x6, starting transfers between devices: 8.09 us -> 10 us  [from_partner(): lax.ppermute(array, axis, [(i, i ^ 1 << stride) for i in range(lax.axis_s...]
    ppermute x4 -> x6, waiting for transfers between devices: 30.1 us -> 31.9 us  [from_partner(): lax.ppermute(array, axis, [(i, i ^ 1 << stride) for i in range(lax.axis_s...]
    dot_general x2, matrix products: 2.05 us -> 0.69 us  [project(): jnp.einsum('rk,rm->km', basis, field.astype(jnp.bfloat16), preferred_elem...]
    unnamed x20 -> x18, local copies, waits for them, and re-layouts: 3.77 us -> 3.78 us
  transfers between devices with their start and end apart: 6 -> 6, of which waited for: 6 -> 6; matrix products, arithmetic and copies ran while one was open for 0% -> 1% of each run, Pallas kernels for 0% -> 0%
where the time goes in v1:
time: 55.5 us; the launch traced here: 55.1 us
  waiting for transfers between devices  31.9 us (57%)
  starting transfers between devices  10 us (18%)
  matrix products  6.61 us (12%)
  local copies, waits for them, and re-layouts  5.17 us (9%)
  other arithmetic  1.16 us (2%)
    ppermute x6, waiting for transfers between devices, from_partner(): lax.ppermute(array, axis, [(i, i ^ 1 << stride) for i in range(lax.axis_s...  31.9 us
    ppermute x6, starting transfers between devices, from_partner(): lax.ppermute(array, axis, [(i, i ^ 1 << stride) for i in range(lax.axis_s...  10 us
    unnamed x18, local copies, waits for them, and re-layouts  3.78 us
    dot_general x1, matrix products, per_device(): jnp.einsum('lij,ljm->lim', leaf_inverse.reshape(leaves, leaf_order, leaf_...  1.53 us
    dot_general x1, matrix products, per_device(): jnp.einsum('ncrk,nckm->ncrm', blocks, coefficients, preferred_element_typ...  1.43 us
  transfers between devices with their start and end apart: 6, of which 6 were waited for; matrix products, arithmetic and copies ran while one was open for 1% of the time, Pallas kernels for 0%

profile of v1, /device:TPU:0, one launch (start us, length us, event | category | flops | bytes accessed | tf_op | source)
XLA Modules:
  0.0 55.1 jit_solution(17077415435316683293)
XLA Ops:
  0.0 1.2 %copy-done = bf16[1024,512]{1,0:T(8,128)(2,1)S(1)} copy-done((bf16[1024,512]{1,0:T(8,128)(2,1)S(1)}, bf16[1024,512]{1,0:T(8,128)(2,1)}, u32[]{:S(2)}) %copy-start) | copy-done | bytes 1048600
  1.2 1.5 %fusion.22 = f32[2,512,256]{2,1,0:T(8,128)S(1)} fusion(bf16[2,512,512]{2,1,0:T(8,128)(2,1)S(1)} %bitcast.43, bf16[2,512,256]{2,1,0:T(8,128)(2,1)} %bitcast.49), kind=kOutput, calls=%fused_computation.34 | convolution fusion | flops 268435456 | bytes 2621440 | tf_op jit(solution)/shard_map/lij,ljm->lim/dot_general | solution.py:62
  2.8 0.3 fusion.13
  3.1 0.7 %copy-done.6 = bf16[512,512]{1,0:T(8,128)(2,1)S(1)} copy-done((bf16[512,512]{1,0:T(8,128)(2,1)S(1)}, bf16[512,512]{1,0:T(8,128)(2,1)}, u32[]{:S(2)}) %copy-start.6) | copy-done | bytes 524312
  3.8 1.0 %fusion.4 = bf16[1,512,256]{1,2,0:T(8,128)(2,1)S(1)} fusion(f32[512,256]{1,0:T(8,128)S(1)} %bitcast.46, bf16[512,512]{1,0:T(8,128)(2,1)S(1)} %copy-done.6), kind=kOutput, calls=%fused_computation.8 | convolution fusion | flops 805437440 | bytes 1310720 | tf_op jit(solution)/shard_map/ij,njm->nim/dot_general | solution.py:75
  5.0 1.4 %fusion.2 = f32[2,512,256]{2,1,0:T(8,128)S(1)} fusion(f32[2,512,256]{2,1,0:T(8,128)S(1)} %fusion.22, bf16[2,512,256]{2,1,0:T(8,128)(2,1)} %bitcast.47, bf16[2,256,256]{1,0,2:T(2,128)(2,1)S(1)} %reshape.41), kind=kOutput, calls=%fused_computation.5 | convolution fusion | flops 134479872 | bytes 2883584 | tf_op jit(solution)/shard_map/ncrk,nckm->ncrm/dot_general | solution.py:83
  6.8 0.6 %collective-permute-start = (f32[256,256]{1,0:T(8,128)S(1)}, f32[256,256]{1,0:T(8,128)S(1)}, u32[]{:S(2)}, u32[]{:S(2)}) collective-permute-start(f32[256,256]{1,0:T(8,128)S(1)} %convolution_bitcast_fusion.4), channel_id=1, source_target_pairs={{0,1},{1,0},{2,3},{3,2},{4,5},{5,4},{6,7},{7,6},{8,9},{9,8},{10,11... | collective-permute-start | bytes 786440 | tf_op jit(solution)/shard_map/ppermute | solution.py:8
  7.3 1.2 %collective-permute-done = f32[256,256]{1,0:T(8,128)S(1)} collective-permute-done((f32[256,256]{1,0:T(8,128)S(1)}, f32[256,256]{1,0:T(8,128)S(1)}, u32[]{:S(2)}, u32[]{:S(2)}) %collective-permute-start) | collective-permute-done | bytes 262176 | tf_op jit(solution)/shard_map/ppermute | solution.py:8
  8.5 2.9 %collective-permute-start.1 = (f32[256,256]{1,0:T(8,128)S(1)}, f32[256,256]{1,0:T(8,128)}, u32[]{:S(2)}, u32[]{:S(2)}) collective-permute-start(f32[256,256]{1,0:T(8,128)S(1)} %add.29), channel_id=1, source_target_pairs={{0,2},{2,0},{4,6},{6,4},{8,10},{10,8},{12,14},{14,12},{1,3},{3,1},... | collective-permute-start | bytes 786440 | tf_op jit(solution)/shard_map/ppermute | solution.py:8
  11.8 6.3 %collective-permute-done.1 = f32[256,256]{1,0:T(8,128)} collective-permute-done((f32[256,256]{1,0:T(8,128)S(1)}, f32[256,256]{1,0:T(8,128)}, u32[]{:S(2)}, u32[]{:S(2)}) %collective-permute-start.1) | collective-permute-done | bytes 262176 | tf_op jit(solution)/shard_map/ppermute | solution.py:8
  18.1 1.0 %broadcast_select_fusion.3 = (f32[256,256]{1,0:T(8,128)S(1)}, f32[256,256]{1,0:T(8,128)S(1)}) fusion(f32[256,256]{1,0:T(8,128)S(1)} %add.29, f32[256,256]{1,0:T(8,128)} %collective-permute-done.1, pred[]{:T(512)S(6)} %eq.11), kind=kLoop, calls=%fused_computation.29 | loop fusion | flops 131072 | bytes 1048577 | tf_op jit(solution)/shard_map/jit(_where)/select_n | solution.py:29
  19.1 0.4 convolution_convert_fusion.2
  19.6 0.6 %copy-done.4 = bf16[1024,256]{1,0:T(8,128)(2,1)S(1)} copy-done((bf16[1024,256]{1,0:T(8,128)(2,1)S(1)}, bf16[1024,256]{1,0:T(8,128)(2,1)}, u32[]{:S(2)}) %copy-start.4) | copy-done | bytes 524312
  20.5 0.7 %copy-done.1 = bf16[1024,256]{1,0:T(8,128)(2,1)S(1)} copy-done((bf16[1024,256]{1,0:T(8,128)(2,1)S(1)}, bf16[1024,256]{1,0:T(8,128)(2,1)}, u32[]{:S(2)}) %copy-start.1) | copy-done | bytes 524312
  21.6 1.5 %collective-permute-done.2 = f32[256,256]{1,0:T(8,128)S(1)} collective-permute-done((f32[256,256]{1,0:T(8,128)S(1)}, f32[256,256]{1,0:T(8,128)S(1)}, u32[]{:S(2)}, u32[]{:S(2)}) %collective-permute-start.2) | collective-permute-done | bytes 262176 | tf_op jit(solution)/shard_map/ppermute | solution.py:8
  23.2 1.8 %collective-permute-start.3 = (f32[256,256]{1,0:T(8,128)S(1)}, f32[256,256]{1,0:T(8,128)S(1)}, u32[]{:S(2)}, u32[]{:S(2)}) collective-permute-start(f32[256,256]{1,0:T(8,128)S(1)} %add.32), channel_id=1, source_target_pairs={{0,2},{2,0},{4,6},{6,4},{8,10},{10,8},{12,14},{14,12},{1,3},{3,1},... | collective-permute-start | bytes 786440 | tf_op jit(solution)/shard_map/ppermute | solution.py:8
  25.0 6.6 %collective-permute-done.3 = f32[256,256]{1,0:T(8,128)S(1)} collective-permute-done((f32[256,256]{1,0:T(8,128)S(1)}, f32[256,256]{1,0:T(8,128)S(1)}, u32[]{:S(2)}, u32[]{:S(2)}) %collective-permute-start.3) | collective-permute-done | bytes 262176 | tf_op jit(solution)/shard_map/ppermute | solution.py:8
  31.7 1.9 %collective-permute-start.4 = (f32[256,256]{1,0:T(8,128)S(1)}, f32[256,256]{1,0:T(8,128)S(1)}, u32[]{:S(2)}, u32[]{:S(2)}) collective-permute-start(f32[256,256]{1,0:T(8,128)S(1)} %add.33), channel_id=1, source_target_pairs={{0,4},{2,6},{4,0},{6,2},{8,12},{10,14},{12,8},{14,10},{1,5},{3,7},... | collective-permute-start | bytes 786440 | tf_op jit(solution)/shard_map/ppermute | solution.py:8
  33.6 5.8 %collective-permute-done.4 = f32[256,256]{1,0:T(8,128)S(1)} collective-permute-done((f32[256,256]{1,0:T(8,128)S(1)}, f32[256,256]{1,0:T(8,128)S(1)}, u32[]{:S(2)}, u32[]{:S(2)}) %collective-permute-start.4) | collective-permute-done | bytes 262176 | tf_op jit(solution)/shard_map/ppermute | solution.py:8
  39.3 2.8 %collective-permute-start.5 = (f32[256,256]{1,0:T(8,128)S(1)}, f32[256,256]{1,0:T(8,128)S(1)}, u32[]{:S(2)}, u32[]{:S(2)}) collective-permute-start(f32[256,256]{1,0:T(8,128)S(1)} %add.34), channel_id=1, source_target_pairs={{0,8},{2,10},{4,12},{6,14},{8,0},{10,2},{12,4},{14,6},{1,9},{3,11}... | collective-permute-start | bytes 786440 | tf_op jit(solution)/shard_map/ppermute | solution.py:8
  42.2 10.5 %collective-permute-done.5 = f32[256,256]{1,0:T(8,128)S(1)} collective-permute-done((f32[256,256]{1,0:T(8,128)S(1)}, f32[256,256]{1,0:T(8,128)S(1)}, u32[]{:S(2)}, u32[]{:S(2)}) %collective-permute-start.5) | collective-permute-done | bytes 262176 | tf_op jit(solution)/shard_map/ppermute | solution.py:8
  52.7 0.4 convolution_convert_fusion.1
  53.2 0.6 %copy-done.2 = bf16[1024,256]{1,0:T(8,128)(2,1)S(1)} copy-done((bf16[1024,256]{1,0:T(8,128)(2,1)S(1)}, bf16[1024,256]{1,0:T(8,128)(2,1)}, u32[]{:S(2)}) %copy-start.2) | copy-done | bytes 524312
  54.1 1.0 %copy.13 = bf16[1024,256]{1,0:T(8,128)(2,1)} copy(bf16[1024,256]{0,1:T(8,128)(2,1)S(1)} %fusion.3) | data formatting | bytes 1048576 | tf_op jit(solution)/shard_map/convert_element_type | solution.py:103
  (25 shorter events, 2.1 us)
Async XLA Ops:
  0.0 1.2 %copy-start = (bf16[1024,512]{1,0:T(8,128)(2,1)S(1)}, bf16[1024,512]{1,0:T(8,128)(2,1)}, u32[]{:S(2)}) copy-start(bf16[1024,512]{1,0:T(8,128)(2,1)} %param.9) | copy-start | bytes 3145732
  1.2 1.5 %copy-start.5 = (bf16[1024,256]{1,0:T(8,128)(2,1)S(1)}, bf16[1024,256]{1,0:T(8,128)(2,1)}, u32[]{:S(2)}) copy-start(bf16[1024,256]{1,0:T(8,128)(2,1)} %param.10) | copy-start | bytes 1572868
  2.8 1.0 %copy-start.6 = (bf16[512,512]{1,0:T(8,128)(2,1)S(1)}, bf16[512,512]{1,0:T(8,128)(2,1)}, u32[]{:S(2)}) copy-start(bf16[512,512]{1,0:T(8,128)(2,1)} %param.13) | copy-start | bytes 1572868
  4.9 1.5 %copy-start.3 = (bf16[1024,256]{1,0:T(8,128)(2,1)S(1)}, bf16[1024,256]{1,0:T(8,128)(2,1)}, u32[]{:S(2)}) copy-start(bf16[1024,256]{1,0:T(8,128)(2,1)} %param.11) | copy-start | bytes 1572868
  6.8 1.7 %collective-permute-start = (f32[256,256]{1,0:T(8,128)S(1)}, f32[256,256]{1,0:T(8,128)S(1)}, u32[]{:S(2)}, u32[]{:S(2)}) collective-permute-start(f32[256,256]{1,0:T(8,128)S(1)} %convolution_bitcast_fusion.4), channel_id=1, source_target_pairs={{0,1},{1,0},{2,3},{3,2},{4,5},{5,4},{6,7},{7,6},{8,9},{9,8},{10,11... | collective-permute-start | bytes 786440 | tf_op jit(solution)/shard_map/ppermute | solution.py:8
  8.5 9.6 %collective-permute-start.1 = (f32[256,256]{1,0:T(8,128)S(1)}, f32[256,256]{1,0:T(8,128)}, u32[]{:S(2)}, u32[]{:S(2)}) collective-permute-start(f32[256,256]{1,0:T(8,128)S(1)} %add.29), channel_id=1, source_target_pairs={{0,2},{2,0},{4,6},{6,4},{8,10},{10,8},{12,14},{14,12},{1,3},{3,1},... | collective-permute-start | bytes 786440 | tf_op jit(solution)/shard_map/ppermute | solution.py:8
  11.8 7.4 %copy-start.7 = (bf16[512,512]{1,0:T(8,128)(2,1)S(1)}, bf16[512,512]{1,0:T(8,128)(2,1)}, u32[]{:S(2)}) copy-start(bf16[512,512]{1,0:T(8,128)(2,1)} %param.14) | copy-start | bytes 1572868
  19.1 1.0 %copy-start.4 = (bf16[1024,256]{1,0:T(8,128)(2,1)S(1)}, bf16[1024,256]{1,0:T(8,128)(2,1)}, u32[]{:S(2)}) copy-start(bf16[1024,256]{1,0:T(8,128)(2,1)} %param.11) | copy-start | bytes 1572868
  20.2 1.0 %copy-start.1 = (bf16[1024,256]{1,0:T(8,128)(2,1)S(1)}, bf16[1024,256]{1,0:T(8,128)(2,1)}, u32[]{:S(2)}) copy-start(bf16[1024,256]{1,0:T(8,128)(2,1)} %param.12) | copy-start | bytes 1572868
  21.6 1.6 %collective-permute-start.2 = (f32[256,256]{1,0:T(8,128)S(1)}, f32[256,256]{1,0:T(8,128)S(1)}, u32[]{:S(2)}, u32[]{:S(2)}) collective-permute-start(f32[256,256]{1,0:T(8,128)S(1)} %convolution_bitcast_fusion.3), channel_id=1, source_target_pairs={{0,1},{1,0},{2,3},{3,2},{4,5},{5,4},{6,7},{7,6},{8,9},{9,8},{10,11... | collective-permute-start | bytes 786440 | tf_op jit(solution)/shard_map/ppermute | solution.py:8
  23.2 8.4 %collective-permute-start.3 = (f32[256,256]{1,0:T(8,128)S(1)}, f32[256,256]{1,0:T(8,128)S(1)}, u32[]{:S(2)}, u32[]{:S(2)}) collective-permute-start(f32[256,256]{1,0:T(8,128)S(1)} %add.32), channel_id=1, source_target_pairs={{0,2},{2,0},{4,6},{6,4},{8,10},{10,8},{12,14},{14,12},{1,3},{3,1},... | collective-permute-start | bytes 786440 | tf_op jit(solution)/shard_map/ppermute | solution.py:8
  31.7 7.7 %collective-permute-start.4 = (f32[256,256]{1,0:T(8,128)S(1)}, f32[256,256]{1,0:T(8,128)S(1)}, u32[]{:S(2)}, u32[]{:S(2)}) collective-permute-start(f32[256,256]{1,0:T(8,128)S(1)} %add.33), channel_id=1, source_target_pairs={{0,4},{2,6},{4,0},{6,2},{8,12},{10,14},{12,8},{14,10},{1,5},{3,7},... | collective-permute-start | bytes 786440 | tf_op jit(solution)/shard_map/ppermute | solution.py:8
  39.3 13.3 %collective-permute-start.5 = (f32[256,256]{1,0:T(8,128)S(1)}, f32[256,256]{1,0:T(8,128)S(1)}, u32[]{:S(2)}, u32[]{:S(2)}) collective-permute-start(f32[256,256]{1,0:T(8,128)S(1)} %add.34), channel_id=1, source_target_pairs={{0,8},{2,10},{4,12},{6,14},{8,0},{10,2},{12,4},{14,6},{1,9},{3,11}... | collective-permute-start | bytes 786440 | tf_op jit(solution)/shard_map/ppermute | solution.py:8
  42.2 10.6 %copy-start.8 = (bf16[512,512]{1,0:T(8,128)(2,1)S(1)}, bf16[512,512]{1,0:T(8,128)(2,1)}, u32[]{:S(2)}) copy-start(bf16[512,512]{1,0:T(8,128)(2,1)} %param.15) | copy-start | bytes 1572868
  52.7 1.0 %copy-start.2 = (bf16[1024,256]{1,0:T(8,128)(2,1)S(1)}, bf16[1024,256]{1,0:T(8,128)(2,1)}, u32[]{:S(2)}) copy-start(bf16[1024,256]{1,0:T(8,128)(2,1)} %param.12) | copy-start | bytes 1572868

commit v2 on v1

v2 whole, which is shorter than its diff:
```python
import functools

import jax
import jax.numpy as jnp
from jax import lax
from jax.experimental import pallas as pl
from jax.experimental.pallas import tpu as pltpu
from jax.sharding import PartitionSpec as P


F32, BF16 = jnp.float32, jnp.bfloat16
VM = pl.BlockSpec(memory_space=pltpu.VMEM)
HB = pl.BlockSpec(memory_space=pl.ANY)


def nn(a, b):
    return lax.dot_general(a, b, (((1,), (0,)), ((), ())), preferred_element_type=F32)


def nt(a, b):
    return lax.dot_general(a, b, (((1,), (1,)), ((), ())), preferred_element_type=F32)


def tn(a, b):
    return lax.dot_general(a, b, (((0,), (0,)), ((), ())), preferred_element_type=F32)


def split(x, terms):
    parts = []
    for _ in range(terms - 1):
        part = x.astype(BF16)
        parts.append(part)
        x = x - part.astype(F32)
    parts.append(x.astype(BF16))
    return parts


def exact_nt(x, capacity):
    rows = x.shape[0]
    out = nt(jnp.concatenate(split(x, 3), axis=0), capacity)
    return out[:rows] + (out[rows : 2 * rows] + out[2 * rows :])


def partner(array, axis, bit):
    return lax.ppermute(array, axis, [(i, i ^ 1 << bit) for i in range(lax.axis_size(axis))])


def params(kib):
    return pltpu.CompilerParams(vmem_limit_bytes=kib * 1024)


def fetch(pairs, sems):
    copies = [
        pltpu.make_async_copy(src, dst, sems.at[i]) for i, (src, dst) in enumerate(pairs)
    ]
    for copy in copies:
        copy.start()
    return copies


def load_kernel(
    leaf, rhs_hbm, inv_hbm, two_hbm, three_hbm, one_hbm, cap_hbm,
    gram_send, gram_keep, field, two, three, one, cap, rhs, inv, gram, sems,
):
    n = rhs.shape[0]
    leaves = n // leaf
    pairs = []
    for i in range(leaves):
        rows = pl.ds(i * leaf, leaf)
        pairs.append((rhs_hbm.at[rows], rhs.at[rows]))
        pairs.append((inv_hbm.at[rows], inv.at[rows]))
    pairs += [(two_hbm, two), (three_hbm, three), (one_hbm, one), (cap_hbm, cap)]
    copies = fetch(pairs, sems)
    for i in range(leaves):
        rows = pl.ds(i * leaf, leaf)
        copies[2 * i].wait()
        flipped = jnp.transpose(rhs[rows, :])
        copies[2 * i + 1].wait()
        field[:, i * leaf : (i + 1) * leaf] = nt(flipped, inv[rows, :])
    copies[2 * leaves].wait()
    copies[2 * leaves + 1].wait()
    gram[...] = tn(two[...], three[...])
    half = gram_keep.shape[0]
    me = lax.axis_index("sub")
    gram_keep[...] = gram[pl.ds(pl.multiple_of(me * half, half), half), :]
    gram_send[...] = gram[pl.ds(pl.multiple_of((1 - me) * half, half), half), :]
    copies[2 * leaves + 2].wait()
    copies[2 * leaves + 3].wait()


def local_kernel(leaf, field, one, cap, two, three, field_out, send, keep, proj):
    m, n = field.shape
    leaves = n // leaf
    rank = one.shape[1]
    width = m // 4
    fields = [field[:, i * leaf : (i + 1) * leaf] for i in range(leaves)]
    bases = [one[pl.ds(i * leaf, leaf), :] for i in range(leaves)]
    projected = [nn(f.astype(BF16), b) for f, b in zip(fields, bases)]
    for i in range(0, leaves, 2):
        stacked = jnp.concatenate(projected[i : i + 2], axis=1)
        coef = exact_nt(stacked, cap[...]).astype(BF16)
        for j in range(2):
            fields[i + j] = fields[i + j] - nt(coef[:, j * rank : (j + 1) * rank], bases[i + j])
    total = jnp.concatenate(fields, axis=1)
    field_out[...] = total
    high, low = split(total, 2)
    proj[0] = nn(high, two[...])
    proj[1] = nn(high, three[...]) + nn(low, three[...])
    me = lax.axis_index("sub")
    for side in range(2):
        for level in range(2):
            for ref, core in ((keep, me), (send, 1 - me)):
                start = pl.multiple_of(side * 2 * width + core * width, width)
                ref[side, level] = proj[level, pl.ds(start, width), :]


def middle_kernel(
    bit, mine, other, cap, gram_own, gram_far, gram_swap, total_out, coef_own, coef_other, gram
):
    rank = mine.shape[2]
    half = rank // 2
    me = lax.axis_index("sub")
    here = pl.ds(pl.multiple_of(me * half, half), half)
    there = pl.ds(pl.multiple_of((1 - me) * half, half), half)
    for i, part in enumerate((gram_own, gram_far)):
        gram[i, here, :] = part[...]
        gram[i, there, :] = gram_swap[i]
    side = (lax.axis_index("row") >> bit) & 1
    own, far = mine[0], other[0]
    is_first = side == 0
    stacked = jnp.concatenate(
        [jnp.where(is_first, own, far), jnp.where(is_first, far, own)], axis=1
    )
    coef = exact_nt(stacked, cap[...]).astype(BF16)
    left, right = coef[:, :rank].astype(F32), coef[:, rank:].astype(F32)
    c_own = jnp.where(is_first, left, right)
    c_far = jnp.where(is_first, right, left)
    coef_own[...] = c_own
    coef_other[...] = c_far
    total = mine[1] + other[1]
    for i, c in enumerate((c_own, c_far)):
        c = c.astype(BF16)
        for part in split(gram[i], 3):
            total = total - nn(c, part)
    total_out[...] = total


def last_coef_kernel(bit, mine, other, cap, out):
    rank = mine.shape[1]
    side = (lax.axis_index("row") >> bit) & 1
    is_first = side == 0
    own, far = mine[...], other[...]
    stacked = jnp.concatenate(
        [jnp.where(is_first, own, far), jnp.where(is_first, far, own)], axis=1
    )
    rows = cap[pl.ds(pl.multiple_of(side * rank, rank), rank), :]
    out[...] = exact_nt(stacked, rows).astype(BF16).astype(F32)


def gather_coef(bit, own, across, cores, scratch):
    width = own.shape[0]
    me = lax.axis_index("sub")
    side = (lax.axis_index("row") >> bit) & 1

    def put(s, c, value):
        start = pl.multiple_of((s * 2 + c) * width, width)
        scratch[pl.ds(start, width), :] = value.astype(BF16)

    put(side, me, own[...])
    put(1 - side, me, across[...])
    put(side, 1 - me, cores[0])
    put(1 - side, 1 - me, cores[1])


def base_kernel(bit, field, own, across, cores, two, out, scratch):
    gather_coef(bit, own, across, cores, scratch)
    out[...] = jnp.transpose(field[...]) - nt(two[...], scratch[...])


def final_kernel(bit, base, own, across, cores, three, out, scratch):
    gather_coef(bit, own, across, cores, scratch)
    out[...] = (base[...] - nt(three[...], scratch[...])).astype(BF16)


def share(own, across):
    return partner(jnp.stack([own, across]), "sub", 0)


def per_device(
    right_sides,
    leaf_inverse,
    basis_one,
    basis_two,
    basis_three,
    capacity_one,
    capacity_two,
    capacity_three,
):
    n, m = right_sides.shape
    leaf = leaf_inverse.shape[1]
    rank = basis_one.shape[1]
    leaves = n // leaf
    width = m // 4
    row_count = lax.axis_size("row")
    row_index = lax.axis_index("row")
    bit_two = (row_count // 8).bit_length() - 1
    bit_three = (row_count // 2).bit_length() - 1
    side = (row_index >> bit_two) & 1

    gram_send, gram_half, field, two, three, one, cap = pl.pallas_call(
        functools.partial(load_kernel, leaf),
        out_shape=[
            jax.ShapeDtypeStruct((rank // 2, rank), F32),
            jax.ShapeDtypeStruct((rank // 2, rank), F32),
            jax.ShapeDtypeStruct((m, n), F32),
            jax.ShapeDtypeStruct((n, rank), BF16),
            jax.ShapeDtypeStruct((n, rank), BF16),
            jax.ShapeDtypeStruct((n, rank), BF16),
            jax.ShapeDtypeStruct(capacity_one.shape, BF16),
        ],
        in_specs=[pl.BlockSpec(memory_space=pltpu.HBM)] * 6,
        out_specs=[VM] * 7,
        scratch_shapes=[
            pltpu.VMEM((n, m), BF16),
            pltpu.VMEM((n, leaf), BF16),
            pltpu.VMEM((rank, rank), F32),
            pltpu.SemaphoreType.DMA((2 * leaves + 4,)),
        ],
        compiler_params=params(12288),
        name="load",
    )(*(
        pltpu.with_memory_space_constraint(x, pltpu.HBM)
        for x in (right_sides, leaf_inverse, basis_two, basis_three, basis_one, capacity_one)
    ))
    gram_half = gram_half + partner(gram_send, "sub", 0)

    field, send, keep = pl.pallas_call(
        functools.partial(local_kernel, leaf),
        out_shape=[
            jax.ShapeDtypeStruct((m, n), F32),
            jax.ShapeDtypeStruct((2, 2, width, rank), F32),
            jax.ShapeDtypeStruct((2, 2, width, rank), F32),
        ],
        in_specs=[VM] * 5,
        out_specs=[VM, VM, VM],
        scratch_shapes=[pltpu.VMEM((2, m, rank), F32)],
        compiler_params=params(12288),
        name="local",
    )(field, one, cap, two, three)

    both = keep + partner(send, "sub", 0)
    for bit in range(bit_two):
        both = both + partner(both, "row", bit)
        gram_half = gram_half + partner(gram_half, "row", bit)
    gram_far = partner(gram_half, "row", bit_two)
    gram_swap = share(gram_half, gram_far)

    mine = lax.dynamic_index_in_dim(both, side, 0, keepdims=False)
    theirs = lax.dynamic_index_in_dim(both, 1 - side, 0, keepdims=False)
    other = partner(theirs, "row", bit_two)
    piece = jax.ShapeDtypeStruct((width, rank), F32)
    total, two_own, two_far = pl.pallas_call(
        functools.partial(middle_kernel, bit_two),
        out_shape=[piece, piece, piece],
        in_specs=[VM] * 6,
        out_specs=[VM] * 3,
        scratch_shapes=[pltpu.VMEM((2, rank, rank), F32)],
        compiler_params=params(4096),
        name="middle",
    )(mine, other, capacity_two, gram_half, gram_far, gram_swap)

    for bit in range(bit_two + 1, bit_three):
        total = total + partner(total, "row", bit)
    sibling = partner(total, "row", bit_three)

    two_across = partner(two_far, "row", bit_two)
    two_cores = share(two_own, two_across)
    base = pl.pallas_call(
        functools.partial(base_kernel, bit_two),
        out_shape=jax.ShapeDtypeStruct((n, m), F32),
        in_specs=[VM] * 5,
        out_specs=VM,
        scratch_shapes=[pltpu.VMEM((m, rank), BF16)],
        compiler_params=params(8192),
        name="base",
    )(field, two_own, two_across, two_cores, two)

    three_own = pl.pallas_call(
        functools.partial(last_coef_kernel, bit_three),
        out_shape=piece,
        in_specs=[VM] * 3,
        out_specs=VM,
        compiler_params=params(2048),
        name="last_coef",
    )(total, sibling, capacity_three)
    three_across = partner(three_own, "row", bit_two)
    three_cores = share(three_own, three_across)
    return pl.pallas_call(
        functools.partial(final_kernel, bit_two),
        out_shape=jax.ShapeDtypeStruct((n, m), BF16),
        in_specs=[VM] * 5,
        out_specs=VM,
        scratch_shapes=[pltpu.VMEM((m, rank), BF16)],
        compiler_params=params(8192),
        name="final",
    )(base, three_own, three_across, three_cores, three)


def solution(mesh):
    rows = P(("grp", "row", "sub"), None)

    return jax.shard_map(
        per_device,
        mesh=mesh,
        in_specs=(rows,) * 5 + (P("grp", None),) * 3,
        out_specs=rows,
        check_vma=False,
    )
```

time: 55.5 us -> 35.9 us (0.65)
  waiting for transfers between devices: 31.9 us -> 14.5 us
  matrix products: 6.61 us -> 0 us
  Pallas kernels: 0 us -> 6.61 us
  local copies, waits for them, and re-layouts: 5.17 us -> 0.03 us
  starting transfers between devices: 10 us -> 13.7 us
    ppermute x6 -> x11, waiting for transfers between devices: 31.9 us -> 14.5 us  [partner(): lax.ppermute(array, axis, [(i, i ^ 1 << bit) for i in range(lax.axis_size...]
    pallas_call x0 -> x6, Pallas kernels: none -> 6.61 us  [the longest x1 2.59 us: per_device(): pl.pallas_call(functools.partial(load_kernel, leaf), out_shape=[jax.Shape...]
    dot_general x10 -> x0, matrix products: 6.61 us -> none  [the longest x1 1.53 us: per_device(): jnp.einsum('lij,ljm->lim', leaf_inverse.reshape(leaves, leaf_order, leaf_...]
    unnamed x18 -> x4, local copies, waits for them, and re-layouts: 3.78 us -> 0.01 us
    ppermute x6 -> x11, starting transfers between devices: 10 us -> 13.7 us  [partner(): lax.ppermute(array, axis, [(i, i ^ 1 << bit) for i in range(lax.axis_size...]
    select_n x2 -> x0, other arithmetic: 1.02 us -> none  [pair_stack(): first = jnp.where(child_side == 0, own_sum, sibling_sum)]
    convert_element_type x1 -> x0, local copies, waits for them, and re-layouts: 1 us -> none  [per_device(): return field.astype(jnp.bfloat16)]
    another operation x0 -> x3, other arithmetic: none -> 0.74 us  [share(): return partner(jnp.stack([own, across]), 'sub', 0)]
  transfers between devices with their start and end apart: 6 -> 11, of which waited for: 6 -> 6; matrix products, arithmetic and copies ran while one was open for 1% -> 2% of each run, Pallas kernels for 0% -> 6%
where the time goes in v2:
time: 35.9 us; the launch traced here: 35.8 us
  waiting for transfers between devices  14.5 us (40%)
  starting transfers between devices  13.7 us (38%)
  Pallas kernels  6.61 us (18%)
  other arithmetic  0.8 us (2%)
    ppermute x11, waiting for transfers between devices, partner(): lax.ppermute(array, axis, [(i, i ^ 1 << bit) for i in range(lax.axis_size...  14.5 us
    ppermute x11, starting transfers between devices, partner(): lax.ppermute(array, axis, [(i, i ^ 1 << bit) for i in range(lax.axis_size...  13.7 us
    pallas_call x1, Pallas kernels, per_device(): pl.pallas_call(functools.partial(load_kernel, leaf), out_shape=[jax.Shape...  2.59 us
    pallas_call x1, Pallas kernels, per_device(): pl.pallas_call(functools.partial(local_kernel, leaf), out_shape=[jax.Shap...  1.67 us
    pallas_call x1, Pallas kernels, per_device(): pl.pallas_call(functools.partial(final_kernel, bit_two), out_shape=jax.Sh...  1.14 us
    another operation x3, other arithmetic, share(): return partner(jnp.stack([own, across]), 'sub', 0)  0.74 us
  transfers between devices with their start and end apart: 11, of which 6 were waited for; matrix products, arithmetic and copies ran while one was open for 2% of the time, Pallas kernels for 6%

profile of v2, /device:TPU:0, one launch (start us, length us, event | category | flops | bytes accessed | tf_op | source)
XLA Modules:
  0.0 35.8 jit_solution(17819342960081448719)
XLA Ops:
  0.0 2.6 %load.1 = (f32[128,256]{1,0:T(8,128)S(1)}, f32[128,256]{1,0:T(8,128)S(1)}, f32[256,1024]{1,0:T(8,128)S(1)}, bf16[1024,256]{1,0:T(8,128)(2,1)S(1)}, bf16[1024,256...) custom-call(bf16[1024,256]{1,0:T(8,128)(2,1)} %rhs_hbm.1, ...), custom_call_target="tpu_custom_call" | custom-call | tf_op jit(solution)/shard_map/load/pallas_call | solution.py:210
  2.6 0.6 %collective-permute-start.2 = (f32[128,256]{1,0:T(8,128)S(1)}, f32[128,256]{1,0:T(8,128)S(1)}, u32[]{:S(2)}, u32[]{:S(2)}) collective-permute-start(f32[128,256]{1,0:T(8,128)S(1)} %get-tuple-element.27), channel_id=1, source_target_pairs={{0,1},{1,0},{2,3},{3,2},{4,5},{5,4},{6,7},{7,6},{8,9},{9,8},{10,11... | collective-permute-start | bytes 393224 | tf_op jit(solution)/shard_map/ppermute | solution.py:45
  3.2 1.7 %local.1 = (f32[256,1024]{1,0:T(8,128)S(1)}, f32[2,2,64,256]{3,2,1,0:T(8,128)S(1)}, f32[2,2,64,256]{3,2,1,0:T(8,128)S(1)}) custom-call(f32[256,1024]{1,0:T(8,128)S(1)} %get-tuple-element.18.field, bf16[1024,256]{1,0:T(8,128)(2,1)S(1)} %get-tuple-element.19.one, bf16[512,512]{1,0:T(8,128)(2,1)S(1)} %get-tuple-element.20.cap, ...), custom_call_target="tpu_custom_call" | custom-call | tf_op jit(solution)/shard_map/local/pallas_call | solution.py:237
  4.8 0.1 collective-permute-start
  4.9 0.0 collective-permute-done.2
  5.0 3.0 %collective-permute-start.3 = (f32[128,256]{1,0:T(8,128)S(1)}, f32[128,256]{1,0:T(8,128)S(1)}, u32[]{:S(2)}, u32[]{:S(2)}) collective-permute-start(f32[128,256]{1,0:T(8,128)S(1)} %add.20.gram_own), channel_id=1, source_target_pairs={{0,2},{2,0},{4,6},{6,4},{8,10},{10,8},{12,14},{14,12},{1,3},{3,1},... | collective-permute-start | bytes 393224 | tf_op jit(solution)/shard_map/ppermute | solution.py:45
  8.0 3.7 %collective-permute-done.3.gram_far = f32[128,256]{1,0:T(8,128)S(1)} collective-permute-done((f32[128,256]{1,0:T(8,128)S(1)}, f32[128,256]{1,0:T(8,128)S(1)}, u32[]{:S(2)}, u32[]{:S(2)}) %collective-permute-start.3) | collective-permute-done | bytes 131104 | tf_op jit(solution)/shard_map/ppermute | solution.py:45
  11.7 0.7 %pad_maximum_fusion = f32[2,128,256]{2,1,0:T(8,128)} fusion(f32[1,128,256]{2,1,0:T(8,128)S(1)} %bitcast.12, f32[1,128,256]{2,1,0:T(8,128)S(1)} %bitcast.10), kind=kLoop, calls=%fused_computation | loop fusion | flops 65536 | bytes 524288 | tf_op jit(solution)/shard_map/stack | solution.py:186
  12.5 1.8 %collective-permute-start.1 = (f32[2,64,256]{2,1,0:T(8,128)S(1)}, f32[2,64,256]{2,1,0:T(8,128)S(1)}, u32[]{:S(2)}, u32[]{:S(2)}) collective-permute-start(f32[2,64,256]{2,1,0:T(8,128)S(1)} %get-tuple-element.31), channel_id=1, source_target_pairs={{0,2},{2,0},{4,6},{6,4},{8,10},{10,8},{12,14},{14,12},{1,3},{3,1},... | collective-permute-start | bytes 393224 | tf_op jit(solution)/shard_map/ppermute | solution.py:45
  14.3 4.2 %collective-permute-done.1.other = f32[2,64,256]{2,1,0:T(8,128)S(1)} collective-permute-done((f32[2,64,256]{2,1,0:T(8,128)S(1)}, f32[2,64,256]{2,1,0:T(8,128)S(1)}, u32[]{:S(2)}, u32[]{:S(2)}) %collective-permute-start.1) | collective-permute-done | bytes 131104 | tf_op jit(solution)/shard_map/ppermute | solution.py:45
  18.5 0.6 %middle.1 = (f32[64,256]{1,0:T(8,128)S(1)}, f32[64,256]{1,0:T(8,128)S(1)}, f32[64,256]{1,0:T(8,128)S(1)}) custom-call(f32[2,64,256]{2,1,0:T(8,128)S(1)} %get-tuple-element.32.mine, f32[2,64,256]{2,1,0:T(8,128)S(1)} %collective-permute-done.1.other, bf16[512,512]{1,0:T(8,128)(2,1)S(1)} %copy-done, f32[128,256]{1,0:T(8,128)S(1)} %add.20.gram_own, ...), custom_call_target="tpu_custom_call" | custom-call | tf_op jit(solution)/shard_map/middle/pallas_call | solution.py:262
  19.1 1.9 %collective-permute-start.7 = (f32[64,256]{1,0:T(8,128)S(1)}, f32[64,256]{1,0:T(8,128)S(1)}, u32[]{:S(2)}, u32[]{:S(2)}) collective-permute-start(f32[64,256]{1,0:T(8,128)S(1)} %get-tuple-element.30), channel_id=1, source_target_pairs={{0,4},{2,6},{4,0},{6,2},{8,12},{10,14},{12,8},{14,10},{1,5},{3,7},... | collective-permute-start | bytes 196616 | tf_op jit(solution)/shard_map/ppermute | solution.py:45
  21.0 2.4 %collective-permute-done.7 = f32[64,256]{1,0:T(8,128)S(1)} collective-permute-done((f32[64,256]{1,0:T(8,128)S(1)}, f32[64,256]{1,0:T(8,128)S(1)}, u32[]{:S(2)}, u32[]{:S(2)}) %collective-permute-start.7) | collective-permute-done | bytes 65568 | tf_op jit(solution)/shard_map/ppermute | solution.py:45
  23.4 2.9 %collective-permute-start.8 = (f32[64,256]{1,0:T(8,128)S(1)}, f32[64,256]{1,0:T(8,128)S(1)}, u32[]{:S(2)}, u32[]{:S(2)}) collective-permute-start(f32[64,256]{1,0:T(8,128)S(1)} %add.21.mine), channel_id=1, source_target_pairs={{0,8},{2,10},{4,12},{6,14},{8,0},{10,2},{12,4},{14,6},{1,9},{3,11}... | collective-permute-start | bytes 196616 | tf_op jit(solution)/shard_map/ppermute | solution.py:45
  26.3 1.5 %collective-permute-start.5 = (f32[64,256]{1,0:T(8,128)S(1)}, f32[64,256]{1,0:T(8,128)S(1)}, u32[]{:S(2)}, u32[]{:S(2)}) collective-permute-start(f32[64,256]{1,0:T(8,128)S(1)} %get-tuple-element.29), channel_id=1, source_target_pairs={{0,2},{2,0},{4,6},{6,4},{8,10},{10,8},{12,14},{14,12},{1,3},{3,1},... | collective-permute-start | bytes 196616 | tf_op jit(solution)/shard_map/ppermute | solution.py:45
  27.8 0.8 %collective-permute-done.8.other = f32[64,256]{1,0:T(8,128)S(1)} collective-permute-done((f32[64,256]{1,0:T(8,128)S(1)}, f32[64,256]{1,0:T(8,128)S(1)}, u32[]{:S(2)}, u32[]{:S(2)}) %collective-permute-start.8) | collective-permute-done | bytes 65568 | tf_op jit(solution)/shard_map/ppermute | solution.py:45
  28.6 0.3 last_coef.1.own
  28.9 1.8 %collective-permute-start.9 = (f32[64,256]{1,0:T(8,128)S(1)}, f32[64,256]{1,0:T(8,128)S(1)}, u32[]{:S(2)}, u32[]{:S(2)}) collective-permute-start(f32[64,256]{1,0:T(8,128)S(1)} %last_coef.1.own), channel_id=1, source_target_pairs={{0,2},{2,0},{4,6},{6,4},{8,10},{10,8},{12,14},{14,12},{1,3},{3,1},... | collective-permute-start | bytes 196616 | tf_op jit(solution)/shard_map/ppermute | solution.py:45
  30.7 0.1 collective-permute-start.6
  30.8 2.4 %collective-permute-done.9.across = f32[64,256]{1,0:T(8,128)S(1)} collective-permute-done((f32[64,256]{1,0:T(8,128)S(1)}, f32[64,256]{1,0:T(8,128)S(1)}, u32[]{:S(2)}, u32[]{:S(2)}) %collective-permute-start.9) | collective-permute-done | bytes 65568 | tf_op jit(solution)/shard_map/ppermute | solution.py:45
  33.2 0.1 collective-permute-start.10
  33.3 0.4 %base.1 = f32[1024,256]{1,0:T(8,128)S(1)} custom-call(f32[256,1024]{1,0:T(8,128)S(1)} %get-tuple-element.23.field, f32[64,256]{1,0:T(8,128)S(1)} %get-tuple-element.28.own, f32[64,256]{1,0:T(8,128)S(1)} %collective-permute-done.5.across, f32[2,64,256]{2,1,0:T(8,128)S(1)} %collective-permute-done.6.cores, bf16[1024,256]{1,0:T(8,128)(2,1)S(1)} %get-tuple-element.21.two), custom_call_target="tpu_custom_call" | custom-call | tf_op jit(solution)/shard_map/base/pallas_call | solution.py:278
  33.7 0.9 %collective-permute-done.10.cores = f32[2,64,256]{2,1,0:T(8,128)S(1)} collective-permute-done((f32[2,64,256]{2,1,0:T(8,128)S(1)}, f32[2,64,256]{2,1,0:T(8,128)S(1)}, u32[]{:S(2)}, u32[]{:S(2)}) %collective-permute-start.10) | collective-permute-done | bytes 131104 | tf_op jit(solution)/shard_map/ppermute | solution.py:45
  34.7 1.1 %final.1 = bf16[1024,256]{1,0:T(8,128)(2,1)} custom-call(f32[1024,256]{1,0:T(8,128)S(1)} %base.1, f32[64,256]{1,0:T(8,128)S(1)} %last_coef.1.own, f32[64,256]{1,0:T(8,128)S(1)} %collective-permute-done.9.across, f32[2,64,256]{2,1,0:T(8,128)S(1)} %collective-permute-done.10.cores, bf16[1024,256]{1,0:T(8,128)(2,1)S(1)} %get-tuple-element.22.three), custom_call_target="tpu_custom_call" | custom-call | tf_op jit(solution)/shard_map/final/pallas_call | solution.py:298
  (15 shorter events, 0.1 us)
Async XLA Ops:
  2.6 2.3 %collective-permute-start.2 = (f32[128,256]{1,0:T(8,128)S(1)}, f32[128,256]{1,0:T(8,128)S(1)}, u32[]{:S(2)}, u32[]{:S(2)}) collective-permute-start(f32[128,256]{1,0:T(8,128)S(1)} %get-tuple-element.27), channel_id=1, source_target_pairs={{0,1},{1,0},{2,3},{3,2},{4,5},{5,4},{6,7},{7,6},{8,9},{9,8},{10,11... | collective-permute-start | bytes 393224 | tf_op jit(solution)/shard_map/ppermute | solution.py:45
  4.8 7.6 %collective-permute-start = (f32[2,2,64,256]{3,2,1,0:T(8,128)S(1)}, f32[2,2,64,256]{3,2,1,0:T(8,128)S(1)}, u32[]{:S(2)}, u32[]{:S(2)}) collective-permute-start(f32[2,2,64,256]{3,2,1,0:T(8,128)S(1)} %get-tuple-element.25), channel_id=1, source_target_pairs={{0,1},{1,0},{2,3},{3,2},{4,5},{5,4},{6,7},{7,6},{8,9},{9,8},{10,11... | collective-permute-start | bytes 786440 | tf_op jit(solution)/shard_map/ppermute | solution.py:45
  5.0 6.7 %collective-permute-start.3 = (f32[128,256]{1,0:T(8,128)S(1)}, f32[128,256]{1,0:T(8,128)S(1)}, u32[]{:S(2)}, u32[]{:S(2)}) collective-permute-start(f32[128,256]{1,0:T(8,128)S(1)} %add.20.gram_own), channel_id=1, source_target_pairs={{0,2},{2,0},{4,6},{6,4},{8,10},{10,8},{12,14},{14,12},{1,3},{3,1},... | collective-permute-start | bytes 393224 | tf_op jit(solution)/shard_map/ppermute | solution.py:45
  12.4 6.1 %collective-permute-start.4 = (f32[2,128,256]{2,1,0:T(8,128)}, f32[2,128,256]{2,1,0:T(8,128)S(1)}, u32[]{:S(2)}, u32[]{:S(2)}) collective-permute-start(f32[2,128,256]{2,1,0:T(8,128)} %pad_maximum_fusion), channel_id=1, source_target_pairs={{0,1},{1,0},{2,3},{3,2},{4,5},{5,4},{6,7},{7,6},{8,9},{9,8},{10,11... | collective-permute-start | bytes 786440 | tf_op jit(solution)/shard_map/ppermute | solution.py:45
  12.4 6.1 %copy-start = (bf16[512,512]{1,0:T(8,128)(2,1)S(1)}, bf16[512,512]{1,0:T(8,128)(2,1)}, u32[]{:S(2)}) copy-start(bf16[512,512]{1,0:T(8,128)(2,1)} %cap.2) | copy-start | bytes 1572868
  12.5 6.0 %collective-permute-start.1 = (f32[2,64,256]{2,1,0:T(8,128)S(1)}, f32[2,64,256]{2,1,0:T(8,128)S(1)}, u32[]{:S(2)}, u32[]{:S(2)}) collective-permute-start(f32[2,64,256]{2,1,0:T(8,128)S(1)} %get-tuple-element.31), channel_id=1, source_target_pairs={{0,2},{2,0},{4,6},{6,4},{8,10},{10,8},{12,14},{14,12},{1,3},{3,1},... | collective-permute-start | bytes 393224 | tf_op jit(solution)/shard_map/ppermute | solution.py:45
  18.5 10.2 %copy-start.1 = (bf16[512,512]{1,0:T(8,128)(2,1)S(1)}, bf16[512,512]{1,0:T(8,128)(2,1)}, u32[]{:S(2)}) copy-start(bf16[512,512]{1,0:T(8,128)(2,1)} %cap.3) | copy-start | bytes 1572868
  19.1 4.3 %collective-permute-start.7 = (f32[64,256]{1,0:T(8,128)S(1)}, f32[64,256]{1,0:T(8,128)S(1)}, u32[]{:S(2)}, u32[]{:S(2)}) collective-permute-start(f32[64,256]{1,0:T(8,128)S(1)} %get-tuple-element.30), channel_id=1, source_target_pairs={{0,4},{2,6},{4,0},{6,2},{8,12},{10,14},{12,8},{14,10},{1,5},{3,7},... | collective-permute-start | bytes 196616 | tf_op jit(solution)/shard_map/ppermute | solution.py:45
  23.4 5.2 %collective-permute-start.8 = (f32[64,256]{1,0:T(8,128)S(1)}, f32[64,256]{1,0:T(8,128)S(1)}, u32[]{:S(2)}, u32[]{:S(2)}) collective-permute-start(f32[64,256]{1,0:T(8,128)S(1)} %add.21.mine), channel_id=1, source_target_pairs={{0,8},{2,10},{4,12},{6,14},{8,0},{10,2},{12,4},{14,6},{1,9},{3,11}... | collective-permute-start | bytes 196616 | tf_op jit(solution)/shard_map/ppermute | solution.py:45
  26.3 4.4 %collective-permute-start.5 = (f32[64,256]{1,0:T(8,128)S(1)}, f32[64,256]{1,0:T(8,128)S(1)}, u32[]{:S(2)}, u32[]{:S(2)}) collective-permute-start(f32[64,256]{1,0:T(8,128)S(1)} %get-tuple-element.29), channel_id=1, source_target_pairs={{0,2},{2,0},{4,6},{6,4},{8,10},{10,8},{12,14},{14,12},{1,3},{3,1},... | collective-permute-start | bytes 196616 | tf_op jit(solution)/shard_map/ppermute | solution.py:45
  28.9 4.3 %collective-permute-start.9 = (f32[64,256]{1,0:T(8,128)S(1)}, f32[64,256]{1,0:T(8,128)S(1)}, u32[]{:S(2)}, u32[]{:S(2)}) collective-permute-start(f32[64,256]{1,0:T(8,128)S(1)} %last_coef.1.own), channel_id=1, source_target_pairs={{0,2},{2,0},{4,6},{6,4},{8,10},{10,8},{12,14},{14,12},{1,3},{3,1},... | collective-permute-start | bytes 196616 | tf_op jit(solution)/shard_map/ppermute | solution.py:45
  30.7 2.6 %collective-permute-start.6 = (f32[2,64,256]{2,1,0:T(8,128)S(1)}, f32[2,64,256]{2,1,0:T(8,128)S(1)}, u32[]{:S(2)}, u32[]{:S(2)}) collective-permute-start(f32[2,64,256]{2,1,0:T(8,128)S(1)} %pad_maximum_fusion.1), channel_id=1, source_target_pairs={{0,1},{1,0},{2,3},{3,2},{4,5},{5,4},{6,7},{7,6},{8,9},{9,8},{10,11... | collective-permute-start | bytes 393224 | tf_op jit(solution)/shard_map/ppermute | solution.py:45
  33.2 1.4 %collective-permute-start.10 = (f32[2,64,256]{2,1,0:T(8,128)S(1)}, f32[2,64,256]{2,1,0:T(8,128)S(1)}, u32[]{:S(2)}, u32[]{:S(2)}) collective-permute-start(f32[2,64,256]{2,1,0:T(8,128)S(1)} %pad_maximum_fusion.2), channel_id=1, source_target_pairs={{0,1},{1,0},{2,3},{3,2},{4,5},{5,4},{6,7},{7,6},{8,9},{9,8},{10,11... | collective-permute-start | bytes 393224 | tf_op jit(solution)/shard_map/ppermute | solution.py:45

commit v3 on v2

--- a/solution.py
+++ b/solution.py
@@ -60,9 +60,10 @@
 
 def load_kernel(
     leaf, rhs_hbm, inv_hbm, two_hbm, three_hbm, one_hbm, cap_hbm,
-    gram_send, gram_keep, field, two, three, one, cap, rhs, inv, gram, sems,
+    gram_send, gram_keep, field, coef, two, three, one, cap, rhs, inv, gram, sems,
 ):
     n = rhs.shape[0]
+    rank = one.shape[1]
     leaves = n // leaf
     pairs = []
     for i in range(leaves):
@@ -71,12 +72,14 @@
         pairs.append((inv_hbm.at[rows], inv.at[rows]))
     pairs += [(two_hbm, two), (three_hbm, three), (one_hbm, one), (cap_hbm, cap)]
     copies = fetch(pairs, sems)
+    fields = []
     for i in range(leaves):
         rows = pl.ds(i * leaf, leaf)
         copies[2 * i].wait()
         flipped = jnp.transpose(rhs[rows, :])
         copies[2 * i + 1].wait()
-        field[:, i * leaf : (i + 1) * leaf] = nt(flipped, inv[rows, :])
+        fields.append(nt(flipped, inv[rows, :]))
+        field[:, i * leaf : (i + 1) * leaf] = fields[i]
     copies[2 * leaves].wait()
     copies[2 * leaves + 1].wait()
     gram[...] = tn(two[...], three[...])
@@ -85,27 +88,33 @@
     gram_keep[...] = gram[pl.ds(pl.multiple_of(me * half, half), half), :]
     gram_send[...] = gram[pl.ds(pl.multiple_of((1 - me) * half, half), half), :]
     copies[2 * leaves + 2].wait()
+    projected = [
+        nn(f.astype(BF16), one[pl.ds(i * leaf, leaf), :]) for i, f in enumerate(fields)
+    ]
     copies[2 * leaves + 3].wait()
-
-
-def local_kernel(leaf, field, one, cap, two, three, field_out, send, keep, proj):
+    for i in range(0, leaves, 2):
+        stacked = jnp.concatenate(projected[i : i + 2], axis=1)
+        coef[:, i * rank : (i + 2) * rank] = exact_nt(stacked, cap[...]).astype(BF16)
+
+
+def local_kernel(leaf, field, coef, one, two, three, field_out, send, keep, proj):
     m, n = field.shape
     leaves = n // leaf
     rank = one.shape[1]
     width = m // 4
-    fields = [field[:, i * leaf : (i + 1) * leaf] for i in range(leaves)]
-    bases = [one[pl.ds(i * leaf, leaf), :] for i in range(leaves)]
-    projected = [nn(f.astype(BF16), b) for f, b in zip(fields, bases)]
-    for i in range(0, leaves, 2):
-        stacked = jnp.concatenate(projected[i : i + 2], axis=1)
-        coef = exact_nt(stacked, cap[...]).astype(BF16)
-        for j in range(2):
-            fields[i + j] = fields[i + j] - nt(coef[:, j * rank : (j + 1) * rank], bases[i + j])
-    total = jnp.concatenate(fields, axis=1)
+    total = jnp.concatenate(
+        [
+            field[:, i * leaf : (i + 1) * leaf]
+            - nt(coef[:, i * rank : (i + 1) * rank], one[pl.ds(i * leaf, leaf), :])
+            for i in range(leaves)
+        ],
+        axis=1,
+    )
     field_out[...] = total
     high, low = split(total, 2)
     proj[0] = nn(high, two[...])
-    proj[1] = nn(high, three[...]) + nn(low, three[...])
+    both = nn(jnp.concatenate([high, low], axis=0), three[...])
+    proj[1] = both[:m] + both[m:]
     me = lax.axis_index("sub")
     for side in range(2):
         for level in range(2):
@@ -177,9 +186,18 @@
     out[...] = jnp.transpose(field[...]) - nt(two[...], scratch[...])
 
 
-def final_kernel(bit, base, own, across, cores, three, out, scratch):
+def final_kernel(bit, base, own, across, cores, three, out_hbm, scratch, out, sems):
     gather_coef(bit, own, across, cores, scratch)
-    out[...] = (base[...] - nt(three[...], scratch[...])).astype(BF16)
+    chunks = sems.shape[0]
+    size = out.shape[0] // chunks
+    copies = []
+    for i in range(chunks):
+        rows = pl.ds(i * size, size)
+        out[rows, :] = (base[rows, :] - nt(three[rows, :], scratch[...])).astype(BF16)
+        copies.append(pltpu.make_async_copy(out.at[rows], out_hbm.at[rows], sems.at[i]))
+        copies[-1].start()
+    for copy in copies:
+        copy.wait()
 
 
 def share(own, across):
@@ -207,20 +225,21 @@
     bit_three = (row_count // 2).bit_length() - 1
     side = (row_index >> bit_two) & 1
 
-    gram_send, gram_half, field, two, three, one, cap = pl.pallas_call(
+    gram_send, gram_half, field, coef, two, three, one = pl.pallas_call(
         functools.partial(load_kernel, leaf),
         out_shape=[
             jax.ShapeDtypeStruct((rank // 2, rank), F32),
             jax.ShapeDtypeStruct((rank // 2, rank), F32),
             jax.ShapeDtypeStruct((m, n), F32),
+            jax.ShapeDtypeStruct((m, leaves * rank), BF16),
             jax.ShapeDtypeStruct((n, rank), BF16),
             jax.ShapeDtypeStruct((n, rank), BF16),
             jax.ShapeDtypeStruct((n, rank), BF16),
-            jax.ShapeDtypeStruct(capacity_one.shape, BF16),
         ],
         in_specs=[pl.BlockSpec(memory_space=pltpu.HBM)] * 6,
         out_specs=[VM] * 7,
         scratch_shapes=[
+            pltpu.VMEM(capacity_one.shape, BF16),
             pltpu.VMEM((n, m), BF16),
             pltpu.VMEM((n, leaf), BF16),
             pltpu.VMEM((rank, rank), F32),
@@ -242,11 +261,11 @@
             jax.ShapeDtypeStruct((2, 2, width, rank), F32),
         ],
         in_specs=[VM] * 5,
-        out_specs=[VM, VM, VM],
+        out_specs=[VM] * 3,
         scratch_shapes=[pltpu.VMEM((2, m, rank), F32)],
-        compiler_params=params(12288),
+        compiler_params=params(8192),
         name="local",
-    )(field, one, cap, two, three)
+    )(field, coef, one, two, three)
 
     both = keep + partner(send, "sub", 0)
     for bit in range(bit_two):
@@ -299,8 +318,12 @@
         functools.partial(final_kernel, bit_two),
         out_shape=jax.ShapeDtypeStruct((n, m), BF16),
         in_specs=[VM] * 5,
-        out_specs=VM,
-        scratch_shapes=[pltpu.VMEM((m, rank), BF16)],
+        out_specs=HB,
+        scratch_shapes=[
+            pltpu.VMEM((m, rank), BF16),
+            pltpu.VMEM((n, m), BF16),
+            pltpu.SemaphoreType.DMA((4,)),
+        ],
         compiler_params=params(8192),
         name="final",
     )(base, three_own, three_across, three_cores, three)

time: 35.9 us -> 36 us (level)
    pallas_call x1, Pallas kernels: 2.59 us -> 3.49 us  [per_device(): pl.pallas_call(functools.partial(load_kernel, leaf), out_shape=[jax.Shape...]
    pallas_call x1, Pallas kernels: 1.67 us -> 0.87 us  [per_device(): pl.pallas_call(functools.partial(local_kernel, leaf), out_shape=[jax.Shap...]
  transfers between devices with their start and end apart: 11 -> 11, of which waited for: 6 -> 6; matrix products, arithmetic and copies ran while one was open for 2% -> 2% of each run, Pallas kernels for 6% -> 4%
where the time goes in v3:
time: 36 us; the launch traced here: 35.8 us
  waiting for transfers between devices  14.5 us (40%)
  starting transfers between devices  13.7 us (38%)
  Pallas kernels  6.68 us (19%)
  other arithmetic  0.8 us (2%)
    ppermute x11, waiting for transfers between devices, partner(): lax.ppermute(array, axis, [(i, i ^ 1 << bit) for i in range(lax.axis_size...  14.5 us
    ppermute x11, starting transfers between devices, partner(): lax.ppermute(array, axis, [(i, i ^ 1 << bit) for i in range(lax.axis_size...  13.7 us
    pallas_call x1, Pallas kernels, per_device(): pl.pallas_call(functools.partial(load_kernel, leaf), out_shape=[jax.Shape...  3.49 us
    pallas_call x1, Pallas kernels, per_device(): pl.pallas_call(functools.partial(final_kernel, bit_two), out_shape=jax.Sh...  1.11 us
    pallas_call x1, Pallas kernels, per_device(): pl.pallas_call(functools.partial(local_kernel, leaf), out_shape=[jax.Shap...  0.87 us
    another operation x3, other arithmetic, share(): return partner(jnp.stack([own, across]), 'sub', 0)  0.74 us
  transfers between devices with their start and end apart: 11, of which 6 were waited for; matrix products, arithmetic and copies ran while one was open for 2% of the time, Pallas kernels for 4%

profile of v3, /device:TPU:0, one launch (start us, length us, event | category | flops | bytes accessed | tf_op | source)
XLA Modules:
  0.0 35.8 jit_solution(6747972052236033846)
XLA Ops:
  0.0 3.5 %load.1 = (f32[128,256]{1,0:T(8,128)S(1)}, f32[128,256]{1,0:T(8,128)S(1)}, f32[256,1024]{1,0:T(8,128)S(1)}, bf16[256,512]{1,0:T(8,128)(2,1)S(1)}, bf16[1024,256]...) custom-call(bf16[1024,256]{1,0:T(8,128)(2,1)} %rhs_hbm.1, ...), custom_call_target="tpu_custom_call" | custom-call | tf_op jit(solution)/shard_map/load/pallas_call | solution.py:228
  3.5 0.6 %collective-permute-start.2 = (f32[128,256]{1,0:T(8,128)S(1)}, f32[128,256]{1,0:T(8,128)S(1)}, u32[]{:S(2)}, u32[]{:S(2)}) collective-permute-start(f32[128,256]{1,0:T(8,128)S(1)} %get-tuple-element.27), channel_id=1, source_target_pairs={{0,1},{1,0},{2,3},{3,2},{4,5},{5,4},{6,7},{7,6},{8,9},{9,8},{10,11... | collective-permute-start | bytes 393224 | tf_op jit(solution)/shard_map/ppermute | solution.py:45
  4.1 0.9 %local.1 = (f32[256,1024]{1,0:T(8,128)S(1)}, f32[2,2,64,256]{3,2,1,0:T(8,128)S(1)}, f32[2,2,64,256]{3,2,1,0:T(8,128)S(1)}) custom-call(f32[256,1024]{1,0:T(8,128)S(1)} %get-tuple-element.18.field, bf16[256,512]{1,0:T(8,128)(2,1)S(1)} %get-tuple-element.19.coef, bf16[1024,256]{1,0:T(8,128)(2,1)S(1)} %get-tuple-element.20.one, ...), custom_call_target="tpu_custom_call" | custom-call | tf_op jit(solution)/shard_map/local/pallas_call | solution.py:256
  4.9 0.1 collective-permute-start
  5.0 0.0 collective-permute-done.2
  5.1 3.0 %collective-permute-start.3 = (f32[128,256]{1,0:T(8,128)S(1)}, f32[128,256]{1,0:T(8,128)S(1)}, u32[]{:S(2)}, u32[]{:S(2)}) collective-permute-start(f32[128,256]{1,0:T(8,128)S(1)} %add.20.gram_own), channel_id=1, source_target_pairs={{0,2},{2,0},{4,6},{6,4},{8,10},{10,8},{12,14},{14,12},{1,3},{3,1},... | collective-permute-start | bytes 393224 | tf_op jit(solution)/shard_map/ppermute | solution.py:45
  8.1 3.7 %collective-permute-done.3.gram_far = f32[128,256]{1,0:T(8,128)S(1)} collective-permute-done((f32[128,256]{1,0:T(8,128)S(1)}, f32[128,256]{1,0:T(8,128)S(1)}, u32[]{:S(2)}, u32[]{:S(2)}) %collective-permute-start.3) | collective-permute-done | bytes 131104 | tf_op jit(solution)/shard_map/ppermute | solution.py:45
  11.8 0.7 %pad_maximum_fusion = f32[2,128,256]{2,1,0:T(8,128)} fusion(f32[1,128,256]{2,1,0:T(8,128)S(1)} %bitcast.12, f32[1,128,256]{2,1,0:T(8,128)S(1)} %bitcast.10), kind=kLoop, calls=%fused_computation | loop fusion | flops 65536 | bytes 524288 | tf_op jit(solution)/shard_map/stack | solution.py:204
  12.6 1.8 %collective-permute-start.1 = (f32[2,64,256]{2,1,0:T(8,128)S(1)}, f32[2,64,256]{2,1,0:T(8,128)S(1)}, u32[]{:S(2)}, u32[]{:S(2)}) collective-permute-start(f32[2,64,256]{2,1,0:T(8,128)S(1)} %get-tuple-element.31), channel_id=1, source_target_pairs={{0,2},{2,0},{4,6},{6,4},{8,10},{10,8},{12,14},{14,12},{1,3},{3,1},... | collective-permute-start | bytes 393224 | tf_op jit(solution)/shard_map/ppermute | solution.py:45
  14.4 4.2 %collective-permute-done.1.other = f32[2,64,256]{2,1,0:T(8,128)S(1)} collective-permute-done((f32[2,64,256]{2,1,0:T(8,128)S(1)}, f32[2,64,256]{2,1,0:T(8,128)S(1)}, u32[]{:S(2)}, u32[]{:S(2)}) %collective-permute-start.1) | collective-permute-done | bytes 131104 | tf_op jit(solution)/shard_map/ppermute | solution.py:45
  18.6 0.6 %middle.1 = (f32[64,256]{1,0:T(8,128)S(1)}, f32[64,256]{1,0:T(8,128)S(1)}, f32[64,256]{1,0:T(8,128)S(1)}) custom-call(f32[2,64,256]{2,1,0:T(8,128)S(1)} %get-tuple-element.32.mine, f32[2,64,256]{2,1,0:T(8,128)S(1)} %collective-permute-done.1.other, bf16[512,512]{1,0:T(8,128)(2,1)S(1)} %copy-done, f32[128,256]{1,0:T(8,128)S(1)} %add.20.gram_own, ...), custom_call_target="tpu_custom_call" | custom-call | tf_op jit(solution)/shard_map/middle/pallas_call | solution.py:281
  19.2 1.9 %collective-permute-start.7 = (f32[64,256]{1,0:T(8,128)S(1)}, f32[64,256]{1,0:T(8,128)S(1)}, u32[]{:S(2)}, u32[]{:S(2)}) collective-permute-start(f32[64,256]{1,0:T(8,128)S(1)} %get-tuple-element.30), channel_id=1, source_target_pairs={{0,4},{2,6},{4,0},{6,2},{8,12},{10,14},{12,8},{14,10},{1,5},{3,7},... | collective-permute-start | bytes 196616 | tf_op jit(solution)/shard_map/ppermute | solution.py:45
  21.0 2.4 %collective-permute-done.7 = f32[64,256]{1,0:T(8,128)S(1)} collective-permute-done((f32[64,256]{1,0:T(8,128)S(1)}, f32[64,256]{1,0:T(8,128)S(1)}, u32[]{:S(2)}, u32[]{:S(2)}) %collective-permute-start.7) | collective-permute-done | bytes 65568 | tf_op jit(solution)/shard_map/ppermute | solution.py:45
  23.5 2.9 %collective-permute-start.8 = (f32[64,256]{1,0:T(8,128)S(1)}, f32[64,256]{1,0:T(8,128)S(1)}, u32[]{:S(2)}, u32[]{:S(2)}) collective-permute-start(f32[64,256]{1,0:T(8,128)S(1)} %add.21.mine), channel_id=1, source_target_pairs={{0,8},{2,10},{4,12},{6,14},{8,0},{10,2},{12,4},{14,6},{1,9},{3,11}... | collective-permute-start | bytes 196616 | tf_op jit(solution)/shard_map/ppermute | solution.py:45
  26.4 1.5 %collective-permute-start.5 = (f32[64,256]{1,0:T(8,128)S(1)}, f32[64,256]{1,0:T(8,128)S(1)}, u32[]{:S(2)}, u32[]{:S(2)}) collective-permute-start(f32[64,256]{1,0:T(8,128)S(1)} %get-tuple-element.29), channel_id=1, source_target_pairs={{0,2},{2,0},{4,6},{6,4},{8,10},{10,8},{12,14},{14,12},{1,3},{3,1},... | collective-permute-start | bytes 196616 | tf_op jit(solution)/shard_map/ppermute | solution.py:45
  27.9 0.8 %collective-permute-done.8.other = f32[64,256]{1,0:T(8,128)S(1)} collective-permute-done((f32[64,256]{1,0:T(8,128)S(1)}, f32[64,256]{1,0:T(8,128)S(1)}, u32[]{:S(2)}, u32[]{:S(2)}) %collective-permute-start.8) | collective-permute-done | bytes 65568 | tf_op jit(solution)/shard_map/ppermute | solution.py:45
  28.7 0.2 last_coef.1.own
  29.0 1.8 %collective-permute-start.9 = (f32[64,256]{1,0:T(8,128)S(1)}, f32[64,256]{1,0:T(8,128)S(1)}, u32[]{:S(2)}, u32[]{:S(2)}) collective-permute-start(f32[64,256]{1,0:T(8,128)S(1)} %last_coef.1.own), channel_id=1, source_target_pairs={{0,2},{2,0},{4,6},{6,4},{8,10},{10,8},{12,14},{14,12},{1,3},{3,1},... | collective-permute-start | bytes 196616 | tf_op jit(solution)/shard_map/ppermute | solution.py:45
  30.8 0.1 collective-permute-start.6
  30.9 2.4 %collective-permute-done.9.across = f32[64,256]{1,0:T(8,128)S(1)} collective-permute-done((f32[64,256]{1,0:T(8,128)S(1)}, f32[64,256]{1,0:T(8,128)S(1)}, u32[]{:S(2)}, u32[]{:S(2)}) %collective-permute-start.9) | collective-permute-done | bytes 65568 | tf_op jit(solution)/shard_map/ppermute | solution.py:45
  33.3 0.1 collective-permute-start.10
  33.4 0.4 %base.1 = f32[1024,256]{1,0:T(8,128)S(1)} custom-call(f32[256,1024]{1,0:T(8,128)S(1)} %get-tuple-element.23.field, f32[64,256]{1,0:T(8,128)S(1)} %get-tuple-element.28.own, f32[64,256]{1,0:T(8,128)S(1)} %collective-permute-done.5.across, f32[2,64,256]{2,1,0:T(8,128)S(1)} %collective-permute-done.6.cores, bf16[1024,256]{1,0:T(8,128)(2,1)S(1)} %get-tuple-element.21.two), custom_call_target="tpu_custom_call" | custom-call | tf_op jit(solution)/shard_map/base/pallas_call | solution.py:297
  33.8 1.0 %collective-permute-done.10.cores = f32[2,64,256]{2,1,0:T(8,128)S(1)} collective-permute-done((f32[2,64,256]{2,1,0:T(8,128)S(1)}, f32[2,64,256]{2,1,0:T(8,128)S(1)}, u32[]{:S(2)}, u32[]{:S(2)}) %collective-permute-start.10) | collective-permute-done | bytes 131104 | tf_op jit(solution)/shard_map/ppermute | solution.py:45
  34.7 1.1 %final.1 = bf16[1024,256]{1,0:T(8,128)(2,1)} custom-call(f32[1024,256]{1,0:T(8,128)S(1)} %base.1, f32[64,256]{1,0:T(8,128)S(1)} %last_coef.1.own, f32[64,256]{1,0:T(8,128)S(1)} %collective-permute-done.9.across, f32[2,64,256]{2,1,0:T(8,128)S(1)} %collective-permute-done.10.cores, bf16[1024,256]{1,0:T(8,128)(2,1)S(1)} %get-tuple-element.22.three), custom_call_target="tpu_custom_call" | custom-call | tf_op jit(solution)/shard_map/final/pallas_call | solution.py:317
  (15 shorter events, 0.1 us)
Async XLA Ops:
  3.5 1.5 %collective-permute-start.2 = (f32[128,256]{1,0:T(8,128)S(1)}, f32[128,256]{1,0:T(8,128)S(1)}, u32[]{:S(2)}, u32[]{:S(2)}) collective-permute-start(f32[128,256]{1,0:T(8,128)S(1)} %get-tuple-element.27), channel_id=1, source_target_pairs={{0,1},{1,0},{2,3},{3,2},{4,5},{5,4},{6,7},{7,6},{8,9},{9,8},{10,11... | collective-permute-start | bytes 393224 | tf_op jit(solution)/shard_map/ppermute | solution.py:45
  4.9 7.6 %collective-permute-start = (f32[2,2,64,256]{3,2,1,0:T(8,128)S(1)}, f32[2,2,64,256]{3,2,1,0:T(8,128)S(1)}, u32[]{:S(2)}, u32[]{:S(2)}) collective-permute-start(f32[2,2,64,256]{3,2,1,0:T(8,128)S(1)} %get-tuple-element.25), channel_id=1, source_target_pairs={{0,1},{1,0},{2,3},{3,2},{4,5},{5,4},{6,7},{7,6},{8,9},{9,8},{10,11... | collective-permute-start | bytes 786440 | tf_op jit(solution)/shard_map/ppermute | solution.py:45
  5.1 6.7 %collective-permute-start.3 = (f32[128,256]{1,0:T(8,128)S(1)}, f32[128,256]{1,0:T(8,128)S(1)}, u32[]{:S(2)}, u32[]{:S(2)}) collective-permute-start(f32[128,256]{1,0:T(8,128)S(1)} %add.20.gram_own), channel_id=1, source_target_pairs={{0,2},{2,0},{4,6},{6,4},{8,10},{10,8},{12,14},{14,12},{1,3},{3,1},... | collective-permute-start | bytes 393224 | tf_op jit(solution)/shard_map/ppermute | solution.py:45
  12.5 6.1 %collective-permute-start.4 = (f32[2,128,256]{2,1,0:T(8,128)}, f32[2,128,256]{2,1,0:T(8,128)S(1)}, u32[]{:S(2)}, u32[]{:S(2)}) collective-permute-start(f32[2,128,256]{2,1,0:T(8,128)} %pad_maximum_fusion), channel_id=1, source_target_pairs={{0,1},{1,0},{2,3},{3,2},{4,5},{5,4},{6,7},{7,6},{8,9},{9,8},{10,11... | collective-permute-start | bytes 786440 | tf_op jit(solution)/shard_map/ppermute | solution.py:45
  12.5 6.1 %copy-start = (bf16[512,512]{1,0:T(8,128)(2,1)S(1)}, bf16[512,512]{1,0:T(8,128)(2,1)}, u32[]{:S(2)}) copy-start(bf16[512,512]{1,0:T(8,128)(2,1)} %cap.2) | copy-start | bytes 1572868
  12.6 6.0 %collective-permute-start.1 = (f32[2,64,256]{2,1,0:T(8,128)S(1)}, f32[2,64,256]{2,1,0:T(8,128)S(1)}, u32[]{:S(2)}, u32[]{:S(2)}) collective-permute-start(f32[2,64,256]{2,1,0:T(8,128)S(1)} %get-tuple-element.31), channel_id=1, source_target_pairs={{0,2},{2,0},{4,6},{6,4},{8,10},{10,8},{12,14},{14,12},{1,3},{3,1},... | collective-permute-start | bytes 393224 | tf_op jit(solution)/shard_map/ppermute | solution.py:45
  18.6 10.2 %copy-start.1 = (bf16[512,512]{1,0:T(8,128)(2,1)S(1)}, bf16[512,512]{1,0:T(8,128)(2,1)}, u32[]{:S(2)}) copy-start(bf16[512,512]{1,0:T(8,128)(2,1)} %cap.3) | copy-start | bytes 1572868
  19.2 4.3 %collective-permute-start.7 = (f32[64,256]{1,0:T(8,128)S(1)}, f32[64,256]{1,0:T(8,128)S(1)}, u32[]{:S(2)}, u32[]{:S(2)}) collective-permute-start(f32[64,256]{1,0:T(8,128)S(1)} %get-tuple-element.30), channel_id=1, source_target_pairs={{0,4},{2,6},{4,0},{6,2},{8,12},{10,14},{12,8},{14,10},{1,5},{3,7},... | collective-permute-start | bytes 196616 | tf_op jit(solution)/shard_map/ppermute | solution.py:45
  23.5 5.2 %collective-permute-start.8 = (f32[64,256]{1,0:T(8,128)S(1)}, f32[64,256]{1,0:T(8,128)S(1)}, u32[]{:S(2)}, u32[]{:S(2)}) collective-permute-start(f32[64,256]{1,0:T(8,128)S(1)} %add.21.mine), channel_id=1, source_target_pairs={{0,8},{2,10},{4,12},{6,14},{8,0},{10,2},{12,4},{14,6},{1,9},{3,11}... | collective-permute-start | bytes 196616 | tf_op jit(solution)/shard_map/ppermute | solution.py:45
  26.4 4.4 %collective-permute-start.5 = (f32[64,256]{1,0:T(8,128)S(1)}, f32[64,256]{1,0:T(8,128)S(1)}, u32[]{:S(2)}, u32[]{:S(2)}) collective-permute-start(f32[64,256]{1,0:T(8,128)S(1)} %get-tuple-element.29), channel_id=1, source_target_pairs={{0,2},{2,0},{4,6},{6,4},{8,10},{10,8},{12,14},{14,12},{1,3},{3,1},... | collective-permute-start | bytes 196616 | tf_op jit(solution)/shard_map/ppermute | solution.py:45
  29.0 4.3 %collective-permute-start.9 = (f32[64,256]{1,0:T(8,128)S(1)}, f32[64,256]{1,0:T(8,128)S(1)}, u32[]{:S(2)}, u32[]{:S(2)}) collective-permute-start(f32[64,256]{1,0:T(8,128)S(1)} %last_coef.1.own), channel_id=1, source_target_pairs={{0,2},{2,0},{4,6},{6,4},{8,10},{10,8},{12,14},{14,12},{1,3},{3,1},... | collective-permute-start | bytes 196616 | tf_op jit(solution)/shard_map/ppermute | solution.py:45
  30.8 2.6 %collective-permute-start.6 = (f32[2,64,256]{2,1,0:T(8,128)S(1)}, f32[2,64,256]{2,1,0:T(8,128)S(1)}, u32[]{:S(2)}, u32[]{:S(2)}) collective-permute-start(f32[2,64,256]{2,1,0:T(8,128)S(1)} %pad_maximum_fusion.1), channel_id=1, source_target_pairs={{0,1},{1,0},{2,3},{3,2},{4,5},{5,4},{6,7},{7,6},{8,9},{9,8},{10,11... | collective-permute-start | bytes 393224 | tf_op jit(solution)/shard_map/ppermute | solution.py:45
  33.3 1.4 %collective-permute-start.10 = (f32[2,64,256]{2,1,0:T(8,128)S(1)}, f32[2,64,256]{2,1,0:T(8,128)S(1)}, u32[]{:S(2)}, u32[]{:S(2)}) collective-permute-start(f32[2,64,256]{2,1,0:T(8,128)S(1)} %pad_maximum_fusion.2), channel_id=1, source_target_pairs={{0,1},{1,0},{2,3},{3,2},{4,5},{5,4},{6,7},{7,6},{8,9},{9,8},{10,11... | collective-permute-start | bytes 393224 | tf_op jit(solution)/shard_map/ppermute | solution.py:45

commit v4 on v3

--- a/solution.py
+++ b/solution.py
@@ -37,8 +37,8 @@
 
 def exact_nt(x, capacity):
     rows = x.shape[0]
-    out = nt(jnp.concatenate(split(x, 3), axis=0), capacity)
-    return out[:rows] + (out[rows : 2 * rows] + out[2 * rows :])
+    out = nt(jnp.concatenate(split(x, 2), axis=0), capacity)
+    return out[:rows] + out[rows:]
 
 
 def partner(array, axis, bit):
@@ -70,31 +70,35 @@
         rows = pl.ds(i * leaf, leaf)
         pairs.append((rhs_hbm.at[rows], rhs.at[rows]))
         pairs.append((inv_hbm.at[rows], inv.at[rows]))
-    pairs += [(two_hbm, two), (three_hbm, three), (one_hbm, one), (cap_hbm, cap)]
+    pairs += [(one_hbm, one), (two_hbm, two), (three_hbm, three), (cap_hbm, cap)]
     copies = fetch(pairs, sems)
-    fields = []
-    for i in range(leaves):
+
+    def solve(i):
         rows = pl.ds(i * leaf, leaf)
-        copies[2 * i].wait()
-        flipped = jnp.transpose(rhs[rows, :])
-        copies[2 * i + 1].wait()
-        fields.append(nt(flipped, inv[rows, :]))
-        field[:, i * leaf : (i + 1) * leaf] = fields[i]
-    copies[2 * leaves].wait()
-    copies[2 * leaves + 1].wait()
+        field[:, i * leaf : (i + 1) * leaf] = nt(jnp.transpose(rhs[rows, :]), inv[rows, :])
+
+    def onto_one(i):
+        part = field[:, i * leaf : (i + 1) * leaf].astype(BF16)
+        return nn(part, one[pl.ds(i * leaf, leaf), :])
+
+    for copy in copies[:2]:
+        copy.wait()
+    solve(0)
+    for copy in copies[2 : 2 * leaves + 1]:
+        copy.wait()
+    for i in range(1, leaves):
+        solve(i)
+    projected = [onto_one(i) for i in range(leaves)]
+    for copy in copies[2 * leaves + 1 :]:
+        copy.wait()
     gram[...] = tn(two[...], three[...])
+    for i in range(0, leaves, 2):
+        stacked = jnp.concatenate(projected[i : i + 2], axis=1)
+        coef[:, i * rank : (i + 2) * rank] = exact_nt(stacked, cap[...]).astype(BF16)
     half = gram_keep.shape[0]
     me = lax.axis_index("sub")
     gram_keep[...] = gram[pl.ds(pl.multiple_of(me * half, half), half), :]
     gram_send[...] = gram[pl.ds(pl.multiple_of((1 - me) * half, half), half), :]
-    copies[2 * leaves + 2].wait()
-    projected = [
-        nn(f.astype(BF16), one[pl.ds(i * leaf, leaf), :]) for i, f in enumerate(fields)
-    ]
-    copies[2 * leaves + 3].wait()
-    for i in range(0, leaves, 2):
-        stacked = jnp.concatenate(projected[i : i + 2], axis=1)
-        coef[:, i * rank : (i + 2) * rank] = exact_nt(stacked, cap[...]).astype(BF16)
 
 
 def local_kernel(leaf, field, coef, one, two, three, field_out, send, keep, proj):
@@ -149,7 +153,7 @@
     total = mine[1] + other[1]
     for i, c in enumerate((c_own, c_far)):
         c = c.astype(BF16)
-        for part in split(gram[i], 3):
+        for part in split(gram[i], 2):
             total = total - nn(c, part)
     total_out[...] = total
 

time: 36 us -> 35.1 us (0.975)
  Pallas kernels: 6.68 us -> 5.82 us
    pallas_call x1, Pallas kernels: 3.49 us -> 2.77 us  [per_device(): pl.pallas_call(functools.partial(load_kernel, leaf), out_shape=[jax.Shape...]
where the time goes in v4:
time: 35.1 us; the launch traced here: 35 us
  waiting for transfers between devices  14.5 us (41%)
  starting transfers between devices  13.7 us (39%)
  Pallas kernels  5.82 us (17%)
  other arithmetic  0.8 us (2%)
    ppermute x11, waiting for transfers between devices, partner(): lax.ppermute(array, axis, [(i, i ^ 1 << bit) for i in range(lax.axis_size...  14.5 us
    ppermute x11, starting transfers between devices, partner(): lax.ppermute(array, axis, [(i, i ^ 1 << bit) for i in range(lax.axis_size...  13.7 us
    pallas_call x1, Pallas kernels, per_device(): pl.pallas_call(functools.partial(load_kernel, leaf), out_shape=[jax.Shape...  2.77 us
    pallas_call x1, Pallas kernels, per_device(): pl.pallas_call(functools.partial(final_kernel, bit_two), out_shape=jax.Sh...  1.11 us
    pallas_call x1, Pallas kernels, per_device(): pl.pallas_call(functools.partial(local_kernel, leaf), out_shape=[jax.Shap...  0.87 us
    another operation x3, other arithmetic, share(): return partner(jnp.stack([own, across]), 'sub', 0)  0.74 us
  transfers between devices with their start and end apart: 11, of which 6 were waited for; matrix products, arithmetic and copies ran while one was open for 2% of the time, Pallas kernels for 4%

profile of v4, /device:TPU:0, one launch (start us, length us, event | category | flops | bytes accessed | tf_op | source)
XLA Modules:
  0.0 35.0 jit_solution(7225501162292599631)
XLA Ops:
  0.0 2.8 %load.1 = (f32[128,256]{1,0:T(8,128)S(1)}, f32[128,256]{1,0:T(8,128)S(1)}, f32[256,1024]{1,0:T(8,128)S(1)}, bf16[256,512]{1,0:T(8,128)(2,1)S(1)}, bf16[1024,256]...) custom-call(bf16[1024,256]{1,0:T(8,128)(2,1)} %rhs_hbm.1, ...), custom_call_target="tpu_custom_call" | custom-call | tf_op jit(solution)/shard_map/load/pallas_call | solution.py:232
  2.8 0.6 %collective-permute-start.2 = (f32[128,256]{1,0:T(8,128)S(1)}, f32[128,256]{1,0:T(8,128)S(1)}, u32[]{:S(2)}, u32[]{:S(2)}) collective-permute-start(f32[128,256]{1,0:T(8,128)S(1)} %get-tuple-element.27), channel_id=1, source_target_pairs={{0,1},{1,0},{2,3},{3,2},{4,5},{5,4},{6,7},{7,6},{8,9},{9,8},{10,11... | collective-permute-start | bytes 393224 | tf_op jit(solution)/shard_map/ppermute | solution.py:45
  3.3 0.9 %local.1 = (f32[256,1024]{1,0:T(8,128)S(1)}, f32[2,2,64,256]{3,2,1,0:T(8,128)S(1)}, f32[2,2,64,256]{3,2,1,0:T(8,128)S(1)}) custom-call(f32[256,1024]{1,0:T(8,128)S(1)} %get-tuple-element.18.field, bf16[256,512]{1,0:T(8,128)(2,1)S(1)} %get-tuple-element.19.coef, bf16[1024,256]{1,0:T(8,128)(2,1)S(1)} %get-tuple-element.20.one, ...), custom_call_target="tpu_custom_call" | custom-call | tf_op jit(solution)/shard_map/local/pallas_call | solution.py:260
  4.2 0.1 collective-permute-start
  4.3 0.0 collective-permute-done.2
  4.3 3.0 %collective-permute-start.3 = (f32[128,256]{1,0:T(8,128)S(1)}, f32[128,256]{1,0:T(8,128)S(1)}, u32[]{:S(2)}, u32[]{:S(2)}) collective-permute-start(f32[128,256]{1,0:T(8,128)S(1)} %add.20.gram_own), channel_id=1, source_target_pairs={{0,2},{2,0},{4,6},{6,4},{8,10},{10,8},{12,14},{14,12},{1,3},{3,1},... | collective-permute-start | bytes 393224 | tf_op jit(solution)/shard_map/ppermute | solution.py:45
  7.3 3.7 %collective-permute-done.3.gram_far = f32[128,256]{1,0:T(8,128)S(1)} collective-permute-done((f32[128,256]{1,0:T(8,128)S(1)}, f32[128,256]{1,0:T(8,128)S(1)}, u32[]{:S(2)}, u32[]{:S(2)}) %collective-permute-start.3) | collective-permute-done | bytes 131104 | tf_op jit(solution)/shard_map/ppermute | solution.py:45
  11.0 0.7 %pad_maximum_fusion = f32[2,128,256]{2,1,0:T(8,128)} fusion(f32[1,128,256]{2,1,0:T(8,128)S(1)} %bitcast.12, f32[1,128,256]{2,1,0:T(8,128)S(1)} %bitcast.10), kind=kLoop, calls=%fused_computation | loop fusion | flops 65536 | bytes 524288 | tf_op jit(solution)/shard_map/stack | solution.py:208
  11.9 1.8 %collective-permute-start.1 = (f32[2,64,256]{2,1,0:T(8,128)S(1)}, f32[2,64,256]{2,1,0:T(8,128)S(1)}, u32[]{:S(2)}, u32[]{:S(2)}) collective-permute-start(f32[2,64,256]{2,1,0:T(8,128)S(1)} %get-tuple-element.31), channel_id=1, source_target_pairs={{0,2},{2,0},{4,6},{6,4},{8,10},{10,8},{12,14},{14,12},{1,3},{3,1},... | collective-permute-start | bytes 393224 | tf_op jit(solution)/shard_map/ppermute | solution.py:45
  13.7 4.2 %collective-permute-done.1.other = f32[2,64,256]{2,1,0:T(8,128)S(1)} collective-permute-done((f32[2,64,256]{2,1,0:T(8,128)S(1)}, f32[2,64,256]{2,1,0:T(8,128)S(1)}, u32[]{:S(2)}, u32[]{:S(2)}) %collective-permute-start.1) | collective-permute-done | bytes 131104 | tf_op jit(solution)/shard_map/ppermute | solution.py:45
  17.8 0.5 %middle.1 = (f32[64,256]{1,0:T(8,128)S(1)}, f32[64,256]{1,0:T(8,128)S(1)}, f32[64,256]{1,0:T(8,128)S(1)}) custom-call(f32[2,64,256]{2,1,0:T(8,128)S(1)} %get-tuple-element.32.mine, f32[2,64,256]{2,1,0:T(8,128)S(1)} %collective-permute-done.1.other, bf16[512,512]{1,0:T(8,128)(2,1)S(1)} %copy-done, f32[128,256]{1,0:T(8,128)S(1)} %add.20.gram_own, ...), custom_call_target="tpu_custom_call" | custom-call | tf_op jit(solution)/shard_map/middle/pallas_call | solution.py:285
  18.3 1.9 %collective-permute-start.7 = (f32[64,256]{1,0:T(8,128)S(1)}, f32[64,256]{1,0:T(8,128)S(1)}, u32[]{:S(2)}, u32[]{:S(2)}) collective-permute-start(f32[64,256]{1,0:T(8,128)S(1)} %get-tuple-element.30), channel_id=1, source_target_pairs={{0,4},{2,6},{4,0},{6,2},{8,12},{10,14},{12,8},{14,10},{1,5},{3,7},... | collective-permute-start | bytes 196616 | tf_op jit(solution)/shard_map/ppermute | solution.py:45
  20.2 2.4 %collective-permute-done.7 = f32[64,256]{1,0:T(8,128)S(1)} collective-permute-done((f32[64,256]{1,0:T(8,128)S(1)}, f32[64,256]{1,0:T(8,128)S(1)}, u32[]{:S(2)}, u32[]{:S(2)}) %collective-permute-start.7) | collective-permute-done | bytes 65568 | tf_op jit(solution)/shard_map/ppermute | solution.py:45
  22.7 2.9 %collective-permute-start.8 = (f32[64,256]{1,0:T(8,128)S(1)}, f32[64,256]{1,0:T(8,128)S(1)}, u32[]{:S(2)}, u32[]{:S(2)}) collective-permute-start(f32[64,256]{1,0:T(8,128)S(1)} %add.21.mine), channel_id=1, source_target_pairs={{0,8},{2,10},{4,12},{6,14},{8,0},{10,2},{12,4},{14,6},{1,9},{3,11}... | collective-permute-start | bytes 196616 | tf_op jit(solution)/shard_map/ppermute | solution.py:45
  25.6 1.5 %collective-permute-start.5 = (f32[64,256]{1,0:T(8,128)S(1)}, f32[64,256]{1,0:T(8,128)S(1)}, u32[]{:S(2)}, u32[]{:S(2)}) collective-permute-start(f32[64,256]{1,0:T(8,128)S(1)} %get-tuple-element.29), channel_id=1, source_target_pairs={{0,2},{2,0},{4,6},{6,4},{8,10},{10,8},{12,14},{14,12},{1,3},{3,1},... | collective-permute-start | bytes 196616 | tf_op jit(solution)/shard_map/ppermute | solution.py:45
  27.1 0.8 %collective-permute-done.8.other = f32[64,256]{1,0:T(8,128)S(1)} collective-permute-done((f32[64,256]{1,0:T(8,128)S(1)}, f32[64,256]{1,0:T(8,128)S(1)}, u32[]{:S(2)}, u32[]{:S(2)}) %collective-permute-start.8) | collective-permute-done | bytes 65568 | tf_op jit(solution)/shard_map/ppermute | solution.py:45
  27.9 0.2 last_coef.1.own
  28.1 1.8 %collective-permute-start.9 = (f32[64,256]{1,0:T(8,128)S(1)}, f32[64,256]{1,0:T(8,128)S(1)}, u32[]{:S(2)}, u32[]{:S(2)}) collective-permute-start(f32[64,256]{1,0:T(8,128)S(1)} %last_coef.1.own), channel_id=1, source_target_pairs={{0,2},{2,0},{4,6},{6,4},{8,10},{10,8},{12,14},{14,12},{1,3},{3,1},... | collective-permute-start | bytes 196616 | tf_op jit(solution)/shard_map/ppermute | solution.py:45
  30.0 0.1 collective-permute-start.6
  30.0 2.4 %collective-permute-done.9.across = f32[64,256]{1,0:T(8,128)S(1)} collective-permute-done((f32[64,256]{1,0:T(8,128)S(1)}, f32[64,256]{1,0:T(8,128)S(1)}, u32[]{:S(2)}, u32[]{:S(2)}) %collective-permute-start.9) | collective-permute-done | bytes 65568 | tf_op jit(solution)/shard_map/ppermute | solution.py:45
  32.5 0.1 collective-permute-start.10
  32.6 0.4 %base.1 = f32[1024,256]{1,0:T(8,128)S(1)} custom-call(f32[256,1024]{1,0:T(8,128)S(1)} %get-tuple-element.23.field, f32[64,256]{1,0:T(8,128)S(1)} %get-tuple-element.28.own, f32[64,256]{1,0:T(8,128)S(1)} %collective-permute-done.5.across, f32[2,64,256]{2,1,0:T(8,128)S(1)} %collective-permute-done.6.cores, bf16[1024,256]{1,0:T(8,128)(2,1)S(1)} %get-tuple-element.21.two), custom_call_target="tpu_custom_call" | custom-call | tf_op jit(solution)/shard_map/base/pallas_call | solution.py:301
  32.9 0.9 %collective-permute-done.10.cores = f32[2,64,256]{2,1,0:T(8,128)S(1)} collective-permute-done((f32[2,64,256]{2,1,0:T(8,128)S(1)}, f32[2,64,256]{2,1,0:T(8,128)S(1)}, u32[]{:S(2)}, u32[]{:S(2)}) %collective-permute-start.10) | collective-permute-done | bytes 131104 | tf_op jit(solution)/shard_map/ppermute | solution.py:45
  33.9 1.1 %final.1 = bf16[1024,256]{1,0:T(8,128)(2,1)} custom-call(f32[1024,256]{1,0:T(8,128)S(1)} %base.1, f32[64,256]{1,0:T(8,128)S(1)} %last_coef.1.own, f32[64,256]{1,0:T(8,128)S(1)} %collective-permute-done.9.across, f32[2,64,256]{2,1,0:T(8,128)S(1)} %collective-permute-done.10.cores, bf16[1024,256]{1,0:T(8,128)(2,1)S(1)} %get-tuple-element.22.three), custom_call_target="tpu_custom_call" | custom-call | tf_op jit(solution)/shard_map/final/pallas_call | solution.py:321
  (15 shorter events, 0.1 us)
Async XLA Ops:
  2.8 1.5 %collective-permute-start.2 = (f32[128,256]{1,0:T(8,128)S(1)}, f32[128,256]{1,0:T(8,128)S(1)}, u32[]{:S(2)}, u32[]{:S(2)}) collective-permute-start(f32[128,256]{1,0:T(8,128)S(1)} %get-tuple-element.27), channel_id=1, source_target_pairs={{0,1},{1,0},{2,3},{3,2},{4,5},{5,4},{6,7},{7,6},{8,9},{9,8},{10,11... | collective-permute-start | bytes 393224 | tf_op jit(solution)/shard_map/ppermute | solution.py:45
  4.2 7.6 %collective-permute-start = (f32[2,2,64,256]{3,2,1,0:T(8,128)S(1)}, f32[2,2,64,256]{3,2,1,0:T(8,128)S(1)}, u32[]{:S(2)}, u32[]{:S(2)}) collective-permute-start(f32[2,2,64,256]{3,2,1,0:T(8,128)S(1)} %get-tuple-element.25), channel_id=1, source_target_pairs={{0,1},{1,0},{2,3},{3,2},{4,5},{5,4},{6,7},{7,6},{8,9},{9,8},{10,11... | collective-permute-start | bytes 786440 | tf_op jit(solution)/shard_map/ppermute | solution.py:45
  4.3 6.7 %collective-permute-start.3 = (f32[128,256]{1,0:T(8,128)S(1)}, f32[128,256]{1,0:T(8,128)S(1)}, u32[]{:S(2)}, u32[]{:S(2)}) collective-permute-start(f32[128,256]{1,0:T(8,128)S(1)} %add.20.gram_own), channel_id=1, source_target_pairs={{0,2},{2,0},{4,6},{6,4},{8,10},{10,8},{12,14},{14,12},{1,3},{3,1},... | collective-permute-start | bytes 393224 | tf_op jit(solution)/shard_map/ppermute | solution.py:45
  11.8 6.1 %collective-permute-start.4 = (f32[2,128,256]{2,1,0:T(8,128)}, f32[2,128,256]{2,1,0:T(8,128)S(1)}, u32[]{:S(2)}, u32[]{:S(2)}) collective-permute-start(f32[2,128,256]{2,1,0:T(8,128)} %pad_maximum_fusion), channel_id=1, source_target_pairs={{0,1},{1,0},{2,3},{3,2},{4,5},{5,4},{6,7},{7,6},{8,9},{9,8},{10,11... | collective-permute-start | bytes 786440 | tf_op jit(solution)/shard_map/ppermute | solution.py:45
  11.8 6.1 %copy-start = (bf16[512,512]{1,0:T(8,128)(2,1)S(1)}, bf16[512,512]{1,0:T(8,128)(2,1)}, u32[]{:S(2)}) copy-start(bf16[512,512]{1,0:T(8,128)(2,1)} %cap.2) | copy-start | bytes 1572868
  11.9 6.0 %collective-permute-start.1 = (f32[2,64,256]{2,1,0:T(8,128)S(1)}, f32[2,64,256]{2,1,0:T(8,128)S(1)}, u32[]{:S(2)}, u32[]{:S(2)}) collective-permute-start(f32[2,64,256]{2,1,0:T(8,128)S(1)} %get-tuple-element.31), channel_id=1, source_target_pairs={{0,2},{2,0},{4,6},{6,4},{8,10},{10,8},{12,14},{14,12},{1,3},{3,1},... | collective-permute-start | bytes 393224 | tf_op jit(solution)/shard_map/ppermute | solution.py:45
  17.8 10.1 %copy-start.1 = (bf16[512,512]{1,0:T(8,128)(2,1)S(1)}, bf16[512,512]{1,0:T(8,128)(2,1)}, u32[]{:S(2)}) copy-start(bf16[512,512]{1,0:T(8,128)(2,1)} %cap.3) | copy-start | bytes 1572868
  18.3 4.3 %collective-permute-start.7 = (f32[64,256]{1,0:T(8,128)S(1)}, f32[64,256]{1,0:T(8,128)S(1)}, u32[]{:S(2)}, u32[]{:S(2)}) collective-permute-start(f32[64,256]{1,0:T(8,128)S(1)} %get-tuple-element.30), channel_id=1, source_target_pairs={{0,4},{2,6},{4,0},{6,2},{8,12},{10,14},{12,8},{14,10},{1,5},{3,7},... | collective-permute-start | bytes 196616 | tf_op jit(solution)/shard_map/ppermute | solution.py:45
  22.7 5.2 %collective-permute-start.8 = (f32[64,256]{1,0:T(8,128)S(1)}, f32[64,256]{1,0:T(8,128)S(1)}, u32[]{:S(2)}, u32[]{:S(2)}) collective-permute-start(f32[64,256]{1,0:T(8,128)S(1)} %add.21.mine), channel_id=1, source_target_pairs={{0,8},{2,10},{4,12},{6,14},{8,0},{10,2},{12,4},{14,6},{1,9},{3,11}... | collective-permute-start | bytes 196616 | tf_op jit(solution)/shard_map/ppermute | solution.py:45
  25.6 4.4 %collective-permute-start.5 = (f32[64,256]{1,0:T(8,128)S(1)}, f32[64,256]{1,0:T(8,128)S(1)}, u32[]{:S(2)}, u32[]{:S(2)}) collective-permute-start(f32[64,256]{1,0:T(8,128)S(1)} %get-tuple-element.29), channel_id=1, source_target_pairs={{0,2},{2,0},{4,6},{6,4},{8,10},{10,8},{12,14},{14,12},{1,3},{3,1},... | collective-permute-start | bytes 196616 | tf_op jit(solution)/shard_map/ppermute | solution.py:45
  28.1 4.3 %collective-permute-start.9 = (f32[64,256]{1,0:T(8,128)S(1)}, f32[64,256]{1,0:T(8,128)S(1)}, u32[]{:S(2)}, u32[]{:S(2)}) collective-permute-start(f32[64,256]{1,0:T(8,128)S(1)} %last_coef.1.own), channel_id=1, source_target_pairs={{0,2},{2,0},{4,6},{6,4},{8,10},{10,8},{12,14},{14,12},{1,3},{3,1},... | collective-permute-start | bytes 196616 | tf_op jit(solution)/shard_map/ppermute | solution.py:45
  30.0 2.6 %collective-permute-start.6 = (f32[2,64,256]{2,1,0:T(8,128)S(1)}, f32[2,64,256]{2,1,0:T(8,128)S(1)}, u32[]{:S(2)}, u32[]{:S(2)}) collective-permute-start(f32[2,64,256]{2,1,0:T(8,128)S(1)} %pad_maximum_fusion.1), channel_id=1, source_target_pairs={{0,1},{1,0},{2,3},{3,2},{4,5},{5,4},{6,7},{7,6},{8,9},{9,8},{10,11... | collective-permute-start | bytes 393224 | tf_op jit(solution)/shard_map/ppermute | solution.py:45
  32.5 1.4 %collective-permute-start.10 = (f32[2,64,256]{2,1,0:T(8,128)S(1)}, f32[2,64,256]{2,1,0:T(8,128)S(1)}, u32[]{:S(2)}, u32[]{:S(2)}) collective-permute-start(f32[2,64,256]{2,1,0:T(8,128)S(1)} %pad_maximum_fusion.2), channel_id=1, source_target_pairs={{0,1},{1,0},{2,3},{3,2},{4,5},{5,4},{6,7},{7,6},{8,9},{9,8},{10,11... | collective-permute-start | bytes 393224 | tf_op jit(solution)/shard_map/ppermute | solution.py:45

commit v5 on v4

--- a/solution.py
+++ b/solution.py
@@ -45,6 +45,18 @@
     return lax.ppermute(array, axis, [(i, i ^ 1 << bit) for i in range(lax.axis_size(axis))])
 
 
+def across_chips(array, bit):
+    cores = lax.axis_size("sub")
+    mask = cores << bit | 1
+    count = cores * lax.axis_size("row")
+    return lax.ppermute(array, ("row", "sub"), [(i, i ^ mask) for i in range(count)])
+
+
+def place(bit):
+    side = (lax.axis_index("row") >> bit) & 1
+    return side, lax.axis_index("sub") ^ side
+
+
 def params(kib):
     return pltpu.CompilerParams(vmem_limit_bytes=kib * 1024)
 
@@ -59,7 +71,7 @@
 
 
 def load_kernel(
-    leaf, rhs_hbm, inv_hbm, two_hbm, three_hbm, one_hbm, cap_hbm,
+    leaf, bit, rhs_hbm, inv_hbm, two_hbm, three_hbm, one_hbm, cap_hbm,
     gram_send, gram_keep, field, coef, two, three, one, cap, rhs, inv, gram, sems,
 ):
     n = rhs.shape[0]
@@ -96,12 +108,12 @@
         stacked = jnp.concatenate(projected[i : i + 2], axis=1)
         coef[:, i * rank : (i + 2) * rank] = exact_nt(stacked, cap[...]).astype(BF16)
     half = gram_keep.shape[0]
-    me = lax.axis_index("sub")
+    _, me = place(bit)
     gram_keep[...] = gram[pl.ds(pl.multiple_of(me * half, half), half), :]
     gram_send[...] = gram[pl.ds(pl.multiple_of((1 - me) * half, half), half), :]
 
 
-def local_kernel(leaf, field, coef, one, two, three, field_out, send, keep, proj):
+def local_kernel(leaf, bit, field, coef, one, two, three, field_out, send, keep, proj):
     m, n = field.shape
     leaves = n // leaf
     rank = one.shape[1]
@@ -119,7 +131,7 @@
     proj[0] = nn(high, two[...])
     both = nn(jnp.concatenate([high, low], axis=0), three[...])
     proj[1] = both[:m] + both[m:]
-    me = lax.axis_index("sub")
+    _, me = place(bit)
     for side in range(2):
         for level in range(2):
             for ref, core in ((keep, me), (send, 1 - me)):
@@ -132,13 +144,12 @@
 ):
     rank = mine.shape[2]
     half = rank // 2
-    me = lax.axis_index("sub")
+    side, me = place(bit)
     here = pl.ds(pl.multiple_of(me * half, half), half)
     there = pl.ds(pl.multiple_of((1 - me) * half, half), half)
     for i, part in enumerate((gram_own, gram_far)):
         gram[i, here, :] = part[...]
         gram[i, there, :] = gram_swap[i]
-    side = (lax.axis_index("row") >> bit) & 1
     own, far = mine[0], other[0]
     is_first = side == 0
     stacked = jnp.concatenate(
@@ -172,8 +183,7 @@
 
 def gather_coef(bit, own, across, cores, scratch):
     width = own.shape[0]
-    me = lax.axis_index("sub")
-    side = (lax.axis_index("row") >> bit) & 1
+    side, me = place(bit)
 
     def put(s, c, value):
         start = pl.multiple_of((s * 2 + c) * width, width)
@@ -230,7 +240,7 @@
     side = (row_index >> bit_two) & 1
 
     gram_send, gram_half, field, coef, two, three, one = pl.pallas_call(
-        functools.partial(load_kernel, leaf),
+        functools.partial(load_kernel, leaf, bit_two),
         out_shape=[
             jax.ShapeDtypeStruct((rank // 2, rank), F32),
             jax.ShapeDtypeStruct((rank // 2, rank), F32),
@@ -258,7 +268,7 @@
     gram_half = gram_half + partner(gram_send, "sub", 0)
 
     field, send, keep = pl.pallas_call(
-        functools.partial(local_kernel, leaf),
+        functools.partial(local_kernel, leaf, bit_two),
         out_shape=[
             jax.ShapeDtypeStruct((m, n), F32),
             jax.ShapeDtypeStruct((2, 2, width, rank), F32),
@@ -275,12 +285,12 @@
     for bit in range(bit_two):
         both = both + partner(both, "row", bit)
         gram_half = gram_half + partner(gram_half, "row", bit)
-    gram_far = partner(gram_half, "row", bit_two)
+    gram_far = across_chips(gram_half, bit_two)
     gram_swap = share(gram_half, gram_far)
 
     mine = lax.dynamic_index_in_dim(both, side, 0, keepdims=False)
     theirs = lax.dynamic_index_in_dim(both, 1 - side, 0, keepdims=False)
-    other = partner(theirs, "row", bit_two)
+    other = across_chips(theirs, bit_two)
     piece = jax.ShapeDtypeStruct((width, rank), F32)
     total, two_own, two_far = pl.pallas_call(
         functools.partial(middle_kernel, bit_two),
@@ -296,7 +306,7 @@
         total = total + partner(total, "row", bit)
     sibling = partner(total, "row", bit_three)
 
-    two_across = partner(two_far, "row", bit_two)
+    two_across = across_chips(two_far, bit_two)
     two_cores = share(two_own, two_across)
     base = pl.pallas_call(
         functools.partial(base_kernel, bit_two),
@@ -316,7 +326,7 @@
         compiler_params=params(2048),
         name="last_coef",
     )(total, sibling, capacity_three)
-    three_across = partner(three_own, "row", bit_two)
+    three_across = across_chips(three_own, bit_two)
     three_cores = share(three_own, three_across)
     return pl.pallas_call(
         functools.partial(final_kernel, bit_two),

time: 35.1 us -> 35.3 us (level)
  waiting for transfers between devices: 14.5 us -> 17.4 us
  starting transfers between devices: 13.7 us -> 11.1 us
    ppermute x0 -> x4, waiting for transfers between devices: none -> 11.2 us  [across_chips(): lax.ppermute(array, ('row', 'sub'), [(i, i ^ mask) for i in range(count)])]
    ppermute x11 -> x7, waiting for transfers between devices: 14.5 us -> 6.17 us  [partner(): lax.ppermute(array, axis, [(i, i ^ 1 << bit) for i in range(lax.axis_size...]
    ppermute x11 -> x7, starting transfers between devices: 13.7 us -> 5.99 us  [partner(): lax.ppermute(array, axis, [(i, i ^ 1 << bit) for i in range(lax.axis_size...]
    ppermute x0 -> x4, starting transfers between devices: none -> 5.14 us  [across_chips(): lax.ppermute(array, ('row', 'sub'), [(i, i ^ mask) for i in range(count)])]
  transfers between devices with their start and end apart: 11 -> 11, of which waited for: 6 -> 8; matrix products, arithmetic and copies ran while one was open for 2% -> 2% of each run, Pallas kernels for 4% -> 4%
where the time goes in v5:
time: 35.3 us; the launch traced here: 35.1 us
  waiting for transfers between devices  17.4 us (49%)
  starting transfers between devices  11.1 us (31%)
  Pallas kernels  5.69 us (16%)
  other arithmetic  0.8 us (2%)
    ppermute x4, waiting for transfers between devices, across_chips(): lax.ppermute(array, ('row', 'sub'), [(i, i ^ mask) for i in range(count)])  11.2 us
    ppermute x7, waiting for transfers between devices, partner(): lax.ppermute(array, axis, [(i, i ^ 1 << bit) for i in range(lax.axis_size...  6.17 us
    ppermute x7, starting transfers between devices, partner(): lax.ppermute(array, axis, [(i, i ^ 1 << bit) for i in range(lax.axis_size...  5.99 us
    ppermute x4, starting transfers between devices, across_chips(): lax.ppermute(array, ('row', 'sub'), [(i, i ^ mask) for i in range(count)])  5.14 us
    pallas_call x1, Pallas kernels, per_device(): pl.pallas_call(functools.partial(load_kernel, leaf, bit_two), out_shape=[...  2.72 us
    pallas_call x1, Pallas kernels, per_device(): pl.pallas_call(functools.partial(final_kernel, bit_two), out_shape=jax.Sh...  1.11 us
    pallas_call x1, Pallas kernels, per_device(): pl.pallas_call(functools.partial(local_kernel, leaf, bit_two), out_shape=...  0.79 us
    another operation x3, other arithmetic, share(): return partner(jnp.stack([own, across]), 'sub', 0)  0.74 us
  transfers between devices with their start and end apart: 11, of which 8 were waited for; matrix products, arithmetic and copies ran while one was open for 2% of the time, Pallas kernels for 4%

profile of v5, /device:TPU:0, one launch (start us, length us, event | category | flops | bytes accessed | tf_op | source)
XLA Modules:
  0.0 35.1 jit_solution(12523885473489835260)
XLA Ops:
  0.0 2.7 %load.1 = (f32[128,256]{1,0:T(8,128)S(1)}, f32[128,256]{1,0:T(8,128)S(1)}, f32[256,1024]{1,0:T(8,128)S(1)}, bf16[256,512]{1,0:T(8,128)(2,1)S(1)}, bf16[1024,256]...) custom-call(bf16[1024,256]{1,0:T(8,128)(2,1)} %rhs_hbm.1, ...), custom_call_target="tpu_custom_call" | custom-call | tf_op jit(solution)/shard_map/load/pallas_call | solution.py:242
  2.7 0.6 %collective-permute-start.2 = (f32[128,256]{1,0:T(8,128)S(1)}, f32[128,256]{1,0:T(8,128)S(1)}, u32[]{:S(2)}, u32[]{:S(2)}) collective-permute-start(f32[128,256]{1,0:T(8,128)S(1)} %get-tuple-element.27), channel_id=1, source_target_pairs={{0,1},{1,0},{2,3},{3,2},{4,5},{5,4},{6,7},{7,6},{8,9},{9,8},{10,11... | collective-permute-start | bytes 393224 | tf_op jit(solution)/shard_map/ppermute | solution.py:45
  3.3 0.8 %local.1 = (f32[256,1024]{1,0:T(8,128)S(1)}, f32[2,2,64,256]{3,2,1,0:T(8,128)S(1)}, f32[2,2,64,256]{3,2,1,0:T(8,128)S(1)}) custom-call(f32[256,1024]{1,0:T(8,128)S(1)} %get-tuple-element.18.field, bf16[256,512]{1,0:T(8,128)(2,1)S(1)} %get-tuple-element.19.coef, bf16[1024,256]{1,0:T(8,128)(2,1)S(1)} %get-tuple-element.20.one, ...), custom_call_target="tpu_custom_call" | custom-call | tf_op jit(solution)/shard_map/local/pallas_call | solution.py:270
  4.2 0.1 collective-permute-done.2
  4.3 2.7 %collective-permute-start.3 = (f32[128,256]{1,0:T(8,128)S(1)}, f32[128,256]{1,0:T(8,128)S(1)}, u32[]{:S(2)}, u32[]{:S(2)}) collective-permute-start(f32[128,256]{1,0:T(8,128)S(1)} %add.20.gram_own), channel_id=1, source_target_pairs={{0,3},{1,2},{2,1},{3,0},{4,7},{5,6},{6,5},{7,4},{8,11},{9,10},{10,... | collective-permute-start | bytes 393224 | tf_op jit(solution)/shard_map/ppermute | solution.py:52
  6.9 3.6 %collective-permute-done.3.gram_far = f32[128,256]{1,0:T(8,128)S(1)} collective-permute-done((f32[128,256]{1,0:T(8,128)S(1)}, f32[128,256]{1,0:T(8,128)S(1)}, u32[]{:S(2)}, u32[]{:S(2)}) %collective-permute-start.3) | collective-permute-done | bytes 131104 | tf_op jit(solution)/shard_map/ppermute | solution.py:52
  10.5 0.7 %pad_maximum_fusion = f32[2,128,256]{2,1,0:T(8,128)} fusion(f32[1,128,256]{2,1,0:T(8,128)S(1)} %bitcast.12, f32[1,128,256]{2,1,0:T(8,128)S(1)} %bitcast.10), kind=kLoop, calls=%fused_computation | loop fusion | flops 65536 | bytes 524288 | tf_op jit(solution)/shard_map/stack | solution.py:218
  11.3 0.3 collective-permute-start.4
  11.6 2.1 %collective-permute-start.1 = (f32[2,64,256]{2,1,0:T(8,128)S(1)}, f32[2,64,256]{2,1,0:T(8,128)S(1)}, u32[]{:S(2)}, u32[]{:S(2)}) collective-permute-start(f32[2,64,256]{2,1,0:T(8,128)S(1)} %get-tuple-element.31), channel_id=1, source_target_pairs={{0,3},{1,2},{2,1},{3,0},{4,7},{5,6},{6,5},{7,4},{8,11},{9,10},{10,... | collective-permute-start | bytes 393224 | tf_op jit(solution)/shard_map/ppermute | solution.py:52
  13.7 3.8 %collective-permute-done.1.other = f32[2,64,256]{2,1,0:T(8,128)S(1)} collective-permute-done((f32[2,64,256]{2,1,0:T(8,128)S(1)}, f32[2,64,256]{2,1,0:T(8,128)S(1)}, u32[]{:S(2)}, u32[]{:S(2)}) %collective-permute-start.1) | collective-permute-done | bytes 131104 | tf_op jit(solution)/shard_map/ppermute | solution.py:52
  17.5 0.5 %middle.1 = (f32[64,256]{1,0:T(8,128)S(1)}, f32[64,256]{1,0:T(8,128)S(1)}, f32[64,256]{1,0:T(8,128)S(1)}) custom-call(f32[2,64,256]{2,1,0:T(8,128)S(1)} %get-tuple-element.32.mine, f32[2,64,256]{2,1,0:T(8,128)S(1)} %collective-permute-done.1.other, bf16[512,512]{1,0:T(8,128)(2,1)S(1)} %copy-done, f32[128,256]{1,0:T(8,128)S(1)} %add.20.gram_own, ...), custom_call_target="tpu_custom_call" | custom-call | tf_op jit(solution)/shard_map/middle/pallas_call | solution.py:295
  18.0 1.6 %collective-permute-start.7 = (f32[64,256]{1,0:T(8,128)S(1)}, f32[64,256]{1,0:T(8,128)S(1)}, u32[]{:S(2)}, u32[]{:S(2)}) collective-permute-start(f32[64,256]{1,0:T(8,128)S(1)} %get-tuple-element.30), channel_id=1, source_target_pairs={{0,4},{2,6},{4,0},{6,2},{8,12},{10,14},{12,8},{14,10},{1,5},{3,7},... | collective-permute-start | bytes 196616 | tf_op jit(solution)/shard_map/ppermute | solution.py:45
  19.6 2.7 %collective-permute-done.7 = f32[64,256]{1,0:T(8,128)S(1)} collective-permute-done((f32[64,256]{1,0:T(8,128)S(1)}, f32[64,256]{1,0:T(8,128)S(1)}, u32[]{:S(2)}, u32[]{:S(2)}) %collective-permute-start.7) | collective-permute-done | bytes 65568 | tf_op jit(solution)/shard_map/ppermute | solution.py:45
  22.3 2.8 %collective-permute-start.8 = (f32[64,256]{1,0:T(8,128)S(1)}, f32[64,256]{1,0:T(8,128)S(1)}, u32[]{:S(2)}, u32[]{:S(2)}) collective-permute-start(f32[64,256]{1,0:T(8,128)S(1)} %add.21.mine), channel_id=1, source_target_pairs={{0,8},{2,10},{4,12},{6,14},{8,0},{10,2},{12,4},{14,6},{1,9},{3,11}... | collective-permute-start | bytes 196616 | tf_op jit(solution)/shard_map/ppermute | solution.py:45
  25.1 0.3 collective-permute-start.5
  25.4 2.5 %collective-permute-done.8.other = f32[64,256]{1,0:T(8,128)S(1)} collective-permute-done((f32[64,256]{1,0:T(8,128)S(1)}, f32[64,256]{1,0:T(8,128)S(1)}, u32[]{:S(2)}, u32[]{:S(2)}) %collective-permute-start.8) | collective-permute-done | bytes 65568 | tf_op jit(solution)/shard_map/ppermute | solution.py:45
  27.9 0.2 last_coef.1.own
  28.2 1.2 %collective-permute-done.5.across = f32[64,256]{1,0:T(8,128)S(1)} collective-permute-done((f32[64,256]{1,0:T(8,128)S(1)}, f32[64,256]{1,0:T(8,128)S(1)}, u32[]{:S(2)}, u32[]{:S(2)}) %collective-permute-start.5) | collective-permute-done | bytes 65568 | tf_op jit(solution)/shard_map/ppermute | solution.py:52
  29.4 0.5 %collective-permute-start.6 = (f32[2,64,256]{2,1,0:T(8,128)S(1)}, f32[2,64,256]{2,1,0:T(8,128)S(1)}, u32[]{:S(2)}, u32[]{:S(2)}) collective-permute-start(f32[2,64,256]{2,1,0:T(8,128)S(1)} %pad_maximum_fusion.1), channel_id=1, source_target_pairs={{0,1},{1,0},{2,3},{3,2},{4,5},{5,4},{6,7},{7,6},{8,9},{9,8},{10,11... | collective-permute-start | bytes 393224 | tf_op jit(solution)/shard_map/ppermute | solution.py:45
  29.9 2.7 %collective-permute-done.9.across = f32[64,256]{1,0:T(8,128)S(1)} collective-permute-done((f32[64,256]{1,0:T(8,128)S(1)}, f32[64,256]{1,0:T(8,128)S(1)}, u32[]{:S(2)}, u32[]{:S(2)}) %collective-permute-start.9) | collective-permute-done | bytes 65568 | tf_op jit(solution)/shard_map/ppermute | solution.py:52
  32.6 0.2 collective-permute-start.10
  32.8 0.4 %base.1 = f32[1024,256]{1,0:T(8,128)S(1)} custom-call(f32[256,1024]{1,0:T(8,128)S(1)} %get-tuple-element.23.field, f32[64,256]{1,0:T(8,128)S(1)} %get-tuple-element.28.own, f32[64,256]{1,0:T(8,128)S(1)} %collective-permute-done.5.across, f32[2,64,256]{2,1,0:T(8,128)S(1)} %collective-permute-done.6.cores, bf16[1024,256]{1,0:T(8,128)(2,1)S(1)} %get-tuple-element.21.two), custom_call_target="tpu_custom_call" | custom-call | tf_op jit(solution)/shard_map/base/pallas_call | solution.py:311
  33.1 0.9 %collective-permute-done.10.cores = f32[2,64,256]{2,1,0:T(8,128)S(1)} collective-permute-done((f32[2,64,256]{2,1,0:T(8,128)S(1)}, f32[2,64,256]{2,1,0:T(8,128)S(1)}, u32[]{:S(2)}, u32[]{:S(2)}) %collective-permute-start.10) | collective-permute-done | bytes 131104 | tf_op jit(solution)/shard_map/ppermute | solution.py:45
  34.0 1.1 %final.1 = bf16[1024,256]{1,0:T(8,128)(2,1)} custom-call(f32[1024,256]{1,0:T(8,128)S(1)} %base.1, f32[64,256]{1,0:T(8,128)S(1)} %last_coef.1.own, f32[64,256]{1,0:T(8,128)S(1)} %collective-permute-done.9.across, f32[2,64,256]{2,1,0:T(8,128)S(1)} %collective-permute-done.10.cores, bf16[1024,256]{1,0:T(8,128)(2,1)S(1)} %get-tuple-element.22.three), custom_call_target="tpu_custom_call" | custom-call | tf_op jit(solution)/shard_map/final/pallas_call | solution.py:331
  (15 shorter events, 0.3 us)
Async XLA Ops:
  2.7 1.5 %collective-permute-start.2 = (f32[128,256]{1,0:T(8,128)S(1)}, f32[128,256]{1,0:T(8,128)S(1)}, u32[]{:S(2)}, u32[]{:S(2)}) collective-permute-start(f32[128,256]{1,0:T(8,128)S(1)} %get-tuple-element.27), channel_id=1, source_target_pairs={{0,1},{1,0},{2,3},{3,2},{4,5},{5,4},{6,7},{7,6},{8,9},{9,8},{10,11... | collective-permute-start | bytes 393224 | tf_op jit(solution)/shard_map/ppermute | solution.py:45
  4.1 7.5 %collective-permute-start = (f32[2,2,64,256]{3,2,1,0:T(8,128)S(1)}, f32[2,2,64,256]{3,2,1,0:T(8,128)S(1)}, u32[]{:S(2)}, u32[]{:S(2)}) collective-permute-start(f32[2,2,64,256]{3,2,1,0:T(8,128)S(1)} %get-tuple-element.25), channel_id=1, source_target_pairs={{0,1},{1,0},{2,3},{3,2},{4,5},{5,4},{6,7},{7,6},{8,9},{9,8},{10,11... | collective-permute-start | bytes 786440 | tf_op jit(solution)/shard_map/ppermute | solution.py:45
  4.3 6.2 %collective-permute-start.3 = (f32[128,256]{1,0:T(8,128)S(1)}, f32[128,256]{1,0:T(8,128)S(1)}, u32[]{:S(2)}, u32[]{:S(2)}) collective-permute-start(f32[128,256]{1,0:T(8,128)S(1)} %add.20.gram_own), channel_id=1, source_target_pairs={{0,3},{1,2},{2,1},{3,0},{4,7},{5,6},{6,5},{7,4},{8,11},{9,10},{10,... | collective-permute-start | bytes 393224 | tf_op jit(solution)/shard_map/ppermute | solution.py:52
  11.3 6.2 %collective-permute-start.4 = (f32[2,128,256]{2,1,0:T(8,128)}, f32[2,128,256]{2,1,0:T(8,128)S(1)}, u32[]{:S(2)}, u32[]{:S(2)}) collective-permute-start(f32[2,128,256]{2,1,0:T(8,128)} %pad_maximum_fusion), channel_id=1, source_target_pairs={{0,1},{1,0},{2,3},{3,2},{4,5},{5,4},{6,7},{7,6},{8,9},{9,8},{10,11... | collective-permute-start | bytes 786440 | tf_op jit(solution)/shard_map/ppermute | solution.py:45
  11.6 5.9 %copy-start = (bf16[512,512]{1,0:T(8,128)(2,1)S(1)}, bf16[512,512]{1,0:T(8,128)(2,1)}, u32[]{:S(2)}) copy-start(bf16[512,512]{1,0:T(8,128)(2,1)} %cap.2) | copy-start | bytes 1572868
  11.6 5.8 %collective-permute-start.1 = (f32[2,64,256]{2,1,0:T(8,128)S(1)}, f32[2,64,256]{2,1,0:T(8,128)S(1)}, u32[]{:S(2)}, u32[]{:S(2)}) collective-permute-start(f32[2,64,256]{2,1,0:T(8,128)S(1)} %get-tuple-element.31), channel_id=1, source_target_pairs={{0,3},{1,2},{2,1},{3,0},{4,7},{5,6},{6,5},{7,4},{8,11},{9,10},{10,... | collective-permute-start | bytes 393224 | tf_op jit(solution)/shard_map/ppermute | solution.py:52
  17.5 10.5 %copy-start.1 = (bf16[512,512]{1,0:T(8,128)(2,1)S(1)}, bf16[512,512]{1,0:T(8,128)(2,1)}, u32[]{:S(2)}) copy-start(bf16[512,512]{1,0:T(8,128)(2,1)} %cap.3) | copy-start | bytes 1572868
  18.0 4.3 %collective-permute-start.7 = (f32[64,256]{1,0:T(8,128)S(1)}, f32[64,256]{1,0:T(8,128)S(1)}, u32[]{:S(2)}, u32[]{:S(2)}) collective-permute-start(f32[64,256]{1,0:T(8,128)S(1)} %get-tuple-element.30), channel_id=1, source_target_pairs={{0,4},{2,6},{4,0},{6,2},{8,12},{10,14},{12,8},{14,10},{1,5},{3,7},... | collective-permute-start | bytes 196616 | tf_op jit(solution)/shard_map/ppermute | solution.py:45
  22.3 5.6 %collective-permute-start.8 = (f32[64,256]{1,0:T(8,128)S(1)}, f32[64,256]{1,0:T(8,128)S(1)}, u32[]{:S(2)}, u32[]{:S(2)}) collective-permute-start(f32[64,256]{1,0:T(8,128)S(1)} %add.21.mine), channel_id=1, source_target_pairs={{0,8},{2,10},{4,12},{6,14},{8,0},{10,2},{12,4},{14,6},{1,9},{3,11}... | collective-permute-start | bytes 196616 | tf_op jit(solution)/shard_map/ppermute | solution.py:45
  25.1 4.3 %collective-permute-start.5 = (f32[64,256]{1,0:T(8,128)S(1)}, f32[64,256]{1,0:T(8,128)S(1)}, u32[]{:S(2)}, u32[]{:S(2)}) collective-permute-start(f32[64,256]{1,0:T(8,128)S(1)} %get-tuple-element.29), channel_id=1, source_target_pairs={{0,3},{1,2},{2,1},{3,0},{4,7},{5,6},{6,5},{7,4},{8,11},{9,10},{10,... | collective-permute-start | bytes 196616 | tf_op jit(solution)/shard_map/ppermute | solution.py:52
  28.2 4.4 %collective-permute-start.9 = (f32[64,256]{1,0:T(8,128)S(1)}, f32[64,256]{1,0:T(8,128)S(1)}, u32[]{:S(2)}, u32[]{:S(2)}) collective-permute-start(f32[64,256]{1,0:T(8,128)S(1)} %last_coef.1.own), channel_id=1, source_target_pairs={{0,3},{1,2},{2,1},{3,0},{4,7},{5,6},{6,5},{7,4},{8,11},{9,10},{10,... | collective-permute-start | bytes 196616 | tf_op jit(solution)/shard_map/ppermute | solution.py:52
  29.4 3.3 %collective-permute-start.6 = (f32[2,64,256]{2,1,0:T(8,128)S(1)}, f32[2,64,256]{2,1,0:T(8,128)S(1)}, u32[]{:S(2)}, u32[]{:S(2)}) collective-permute-start(f32[2,64,256]{2,1,0:T(8,128)S(1)} %pad_maximum_fusion.1), channel_id=1, source_target_pairs={{0,1},{1,0},{2,3},{3,2},{4,5},{5,4},{6,7},{7,6},{8,9},{9,8},{10,11... | collective-permute-start | bytes 393224 | tf_op jit(solution)/shard_map/ppermute | solution.py:45
  32.6 1.4 %collective-permute-start.10 = (f32[2,64,256]{2,1,0:T(8,128)S(1)}, f32[2,64,256]{2,1,0:T(8,128)S(1)}, u32[]{:S(2)}, u32[]{:S(2)}) collective-permute-start(f32[2,64,256]{2,1,0:T(8,128)S(1)} %pad_maximum_fusion.2), channel_id=1, source_target_pairs={{0,1},{1,0},{2,3},{3,2},{4,5},{5,4},{6,7},{7,6},{8,9},{9,8},{10,11... | collective-permute-start | bytes 393224 | tf_op jit(solution)/shard_map/ppermute | solution.py:45

commit v6 on v5

--- a/solution.py
+++ b/solution.py
@@ -135,7 +135,7 @@
     for side in range(2):
         for level in range(2):
             for ref, core in ((keep, me), (send, 1 - me)):
-                start = pl.multiple_of(side * 2 * width + core * width, width)
+                start = pl.multiple_of(core * 2 * width + side * width, width)
                 ref[side, level] = proj[level, pl.ds(start, width), :]
 
 
@@ -186,7 +186,7 @@
     side, me = place(bit)
 
     def put(s, c, value):
-        start = pl.multiple_of((s * 2 + c) * width, width)
+        start = pl.multiple_of((c * 2 + s) * width, width)
         scratch[pl.ds(start, width), :] = value.astype(BF16)
 
     put(side, me, own[...])
@@ -200,15 +200,31 @@
     out[...] = jnp.transpose(field[...]) - nt(two[...], scratch[...])
 
 
-def final_kernel(bit, base, own, across, cores, three, out_hbm, scratch, out, sems):
-    gather_coef(bit, own, across, cores, scratch)
-    chunks = sems.shape[0]
+def half_kernel(bit, base, own, across, three, out, scratch):
+    width = own.shape[0]
+    side, me = place(bit)
+    scratch[pl.ds(pl.multiple_of(side * width, width), width), :] = own[...].astype(BF16)
+    scratch[pl.ds(pl.multiple_of((1 - side) * width, width), width), :] = across[...].astype(BF16)
+    columns = pl.ds(pl.multiple_of(me * 2 * width, 2 * width), 2 * width)
+    out[...] = (base[:, columns] - nt(three[...], scratch[...])).astype(BF16)
+
+
+def final_kernel(bit, base, half, cores, three, out_hbm, scratch, out, sems):
+    width = cores.shape[1]
+    side, me = place(bit)
+    mine = pl.ds(pl.multiple_of(me * 2 * width, 2 * width), 2 * width)
+    theirs = pl.ds(pl.multiple_of((1 - me) * 2 * width, 2 * width), 2 * width)
+    copies = [pltpu.make_async_copy(half, out_hbm.at[:, mine], sems.at[0])]
+    copies[0].start()
+    for i in range(2):
+        start = pl.multiple_of((side + i - 2 * side * i) * width, width)
+        scratch[pl.ds(start, width), :] = cores[i].astype(BF16)
+    chunks = sems.shape[0] - 1
     size = out.shape[0] // chunks
-    copies = []
     for i in range(chunks):
         rows = pl.ds(i * size, size)
-        out[rows, :] = (base[rows, :] - nt(three[rows, :], scratch[...])).astype(BF16)
-        copies.append(pltpu.make_async_copy(out.at[rows], out_hbm.at[rows], sems.at[i]))
+        out[rows, :] = (base[rows, theirs] - nt(three[rows, :], scratch[...])).astype(BF16)
+        copies.append(pltpu.make_async_copy(out.at[rows], out_hbm.at[rows, theirs], sems.at[i + 1]))
         copies[-1].start()
     for copy in copies:
         copy.wait()
@@ -328,19 +344,28 @@
     )(total, sibling, capacity_three)
     three_across = across_chips(three_own, bit_two)
     three_cores = share(three_own, three_across)
+    half = pl.pallas_call(
+        functools.partial(half_kernel, bit_two),
+        out_shape=jax.ShapeDtypeStruct((n, 2 * width), BF16),
+        in_specs=[VM] * 4,
+        out_specs=VM,
+        scratch_shapes=[pltpu.VMEM((2 * width, rank), BF16)],
+        compiler_params=params(4096),
+        name="half",
+    )(base, three_own, three_across, three)
     return pl.pallas_call(
         functools.partial(final_kernel, bit_two),
         out_shape=jax.ShapeDtypeStruct((n, m), BF16),
-        in_specs=[VM] * 5,
+        in_specs=[VM] * 4,
         out_specs=HB,
         scratch_shapes=[
-            pltpu.VMEM((m, rank), BF16),
-            pltpu.VMEM((n, m), BF16),
-            pltpu.SemaphoreType.DMA((4,)),
+            pltpu.VMEM((2 * width, rank), BF16),
+            pltpu.VMEM((n, 2 * width), BF16),
+            pltpu.SemaphoreType.DMA((3,)),
         ],
         compiler_params=params(8192),
         name="final",
-    )(base, three_own, three_across, three_cores, three)
+    )(base, half, three_cores, three)
 
 
 def solution(mesh):

time: 35.3 us -> 35.2 us (level)
  waiting for transfers between devices: 17.4 us -> 17 us
  transfers between devices with their start and end apart: 11 -> 11, of which waited for: 8 -> 8; matrix products, arithmetic and copies ran while one was open for 2% -> 2% of each run, Pallas kernels for 4% -> 5%
where the time goes in v6:
time: 35.2 us; the launch traced here: 35 us
  waiting for transfers between devices  17 us (48%)
  starting transfers between devices  11.1 us (32%)
  Pallas kernels  5.94 us (17%)
  other arithmetic  0.8 us (2%)
    ppermute x4, waiting for transfers between devices, across_chips(): lax.ppermute(array, ('row', 'sub'), [(i, i ^ mask) for i in range(count)])  11.2 us
    ppermute x7, starting transfers between devices, partner(): lax.ppermute(array, axis, [(i, i ^ 1 << bit) for i in range(lax.axis_size...  5.99 us
    ppermute x7, waiting for transfers between devices, partner(): lax.ppermute(array, axis, [(i, i ^ 1 << bit) for i in range(lax.axis_size...  5.85 us
    ppermute x4, starting transfers between devices, across_chips(): lax.ppermute(array, ('row', 'sub'), [(i, i ^ mask) for i in range(count)])  5.14 us
    pallas_call x1, Pallas kernels, per_device(): pl.pallas_call(functools.partial(load_kernel, leaf, bit_two), out_shape=[...  2.72 us
    pallas_call x1, Pallas kernels, per_device(): pl.pallas_call(functools.partial(final_kernel, bit_two), out_shape=jax.Sh...  1.03 us
    pallas_call x1, Pallas kernels, per_device(): pl.pallas_call(functools.partial(local_kernel, leaf, bit_two), out_shape=...  0.79 us
    another operation x3, other arithmetic, share(): return partner(jnp.stack([own, across]), 'sub', 0)  0.74 us
  transfers between devices with their start and end apart: 11, of which 8 were waited for; matrix products, arithmetic and copies ran while one was open for 2% of the time, Pallas kernels for 5%

profile of v6, /device:TPU:0, one launch (start us, length us, event | category | flops | bytes accessed | tf_op | source)
XLA Modules:
  0.0 35.0 jit_solution(13757214506908670064)
XLA Ops:
  0.0 2.7 %load.1 = (f32[128,256]{1,0:T(8,128)S(1)}, f32[128,256]{1,0:T(8,128)S(1)}, f32[256,1024]{1,0:T(8,128)S(1)}, bf16[256,512]{1,0:T(8,128)(2,1)S(1)}, bf16[1024,256]...) custom-call(bf16[1024,256]{1,0:T(8,128)(2,1)} %rhs_hbm.1, ...), custom_call_target="tpu_custom_call" | custom-call | tf_op jit(solution)/shard_map/load/pallas_call | solution.py:258
  2.7 0.6 %collective-permute-start.2 = (f32[128,256]{1,0:T(8,128)S(1)}, f32[128,256]{1,0:T(8,128)S(1)}, u32[]{:S(2)}, u32[]{:S(2)}) collective-permute-start(f32[128,256]{1,0:T(8,128)S(1)} %get-tuple-element.27), channel_id=1, source_target_pairs={{0,1},{1,0},{2,3},{3,2},{4,5},{5,4},{6,7},{7,6},{8,9},{9,8},{10,11... | collective-permute-start | bytes 393224 | tf_op jit(solution)/shard_map/ppermute | solution.py:45
  3.3 0.8 %local.1 = (f32[256,1024]{1,0:T(8,128)S(1)}, f32[2,2,64,256]{3,2,1,0:T(8,128)S(1)}, f32[2,2,64,256]{3,2,1,0:T(8,128)S(1)}) custom-call(f32[256,1024]{1,0:T(8,128)S(1)} %get-tuple-element.18.field, bf16[256,512]{1,0:T(8,128)(2,1)S(1)} %get-tuple-element.19.coef, bf16[1024,256]{1,0:T(8,128)(2,1)S(1)} %get-tuple-element.20.one, ...), custom_call_target="tpu_custom_call" | custom-call | tf_op jit(solution)/shard_map/local/pallas_call | solution.py:286
  4.3 2.7 %collective-permute-start.3 = (f32[128,256]{1,0:T(8,128)S(1)}, f32[128,256]{1,0:T(8,128)S(1)}, u32[]{:S(2)}, u32[]{:S(2)}) collective-permute-start(f32[128,256]{1,0:T(8,128)S(1)} %add.20.gram_own), channel_id=1, source_target_pairs={{0,3},{1,2},{2,1},{3,0},{4,7},{5,6},{6,5},{7,4},{8,11},{9,10},{10,... | collective-permute-start | bytes 393224 | tf_op jit(solution)/shard_map/ppermute | solution.py:52
  6.9 3.6 %collective-permute-done.3.gram_far = f32[128,256]{1,0:T(8,128)S(1)} collective-permute-done((f32[128,256]{1,0:T(8,128)S(1)}, f32[128,256]{1,0:T(8,128)S(1)}, u32[]{:S(2)}, u32[]{:S(2)}) %collective-permute-start.3) | collective-permute-done | bytes 131104 | tf_op jit(solution)/shard_map/ppermute | solution.py:52
  10.5 0.7 %pad_maximum_fusion = f32[2,128,256]{2,1,0:T(8,128)} fusion(f32[1,128,256]{2,1,0:T(8,128)S(1)} %bitcast.12, f32[1,128,256]{2,1,0:T(8,128)S(1)} %bitcast.10), kind=kLoop, calls=%fused_computation | loop fusion | flops 65536 | bytes 524288 | tf_op jit(solution)/shard_map/stack | solution.py:234
  11.3 0.3 collective-permute-start.4
  11.6 2.1 %collective-permute-start.1 = (f32[2,64,256]{2,1,0:T(8,128)S(1)}, f32[2,64,256]{2,1,0:T(8,128)S(1)}, u32[]{:S(2)}, u32[]{:S(2)}) collective-permute-start(f32[2,64,256]{2,1,0:T(8,128)S(1)} %get-tuple-element.31), channel_id=1, source_target_pairs={{0,3},{1,2},{2,1},{3,0},{4,7},{5,6},{6,5},{7,4},{8,11},{9,10},{10,... | collective-permute-start | bytes 393224 | tf_op jit(solution)/shard_map/ppermute | solution.py:52
  13.7 3.8 %collective-permute-done.1.other = f32[2,64,256]{2,1,0:T(8,128)S(1)} collective-permute-done((f32[2,64,256]{2,1,0:T(8,128)S(1)}, f32[2,64,256]{2,1,0:T(8,128)S(1)}, u32[]{:S(2)}, u32[]{:S(2)}) %collective-permute-start.1) | collective-permute-done | bytes 131104 | tf_op jit(solution)/shard_map/ppermute | solution.py:52
  17.5 0.5 %middle.1 = (f32[64,256]{1,0:T(8,128)S(1)}, f32[64,256]{1,0:T(8,128)S(1)}, f32[64,256]{1,0:T(8,128)S(1)}) custom-call(f32[2,64,256]{2,1,0:T(8,128)S(1)} %get-tuple-element.32.mine, f32[2,64,256]{2,1,0:T(8,128)S(1)} %collective-permute-done.1.other, bf16[512,512]{1,0:T(8,128)(2,1)S(1)} %copy-done, f32[128,256]{1,0:T(8,128)S(1)} %add.20.gram_own, ...), custom_call_target="tpu_custom_call" | custom-call | tf_op jit(solution)/shard_map/middle/pallas_call | solution.py:311
  18.0 1.6 %collective-permute-start.7 = (f32[64,256]{1,0:T(8,128)S(1)}, f32[64,256]{1,0:T(8,128)S(1)}, u32[]{:S(2)}, u32[]{:S(2)}) collective-permute-start(f32[64,256]{1,0:T(8,128)S(1)} %get-tuple-element.30), channel_id=1, source_target_pairs={{0,4},{2,6},{4,0},{6,2},{8,12},{10,14},{12,8},{14,10},{1,5},{3,7},... | collective-permute-start | bytes 196616 | tf_op jit(solution)/shard_map/ppermute | solution.py:45
  19.6 2.7 %collective-permute-done.7 = f32[64,256]{1,0:T(8,128)S(1)} collective-permute-done((f32[64,256]{1,0:T(8,128)S(1)}, f32[64,256]{1,0:T(8,128)S(1)}, u32[]{:S(2)}, u32[]{:S(2)}) %collective-permute-start.7) | collective-permute-done | bytes 65568 | tf_op jit(solution)/shard_map/ppermute | solution.py:45
  22.3 2.8 %collective-permute-start.8 = (f32[64,256]{1,0:T(8,128)S(1)}, f32[64,256]{1,0:T(8,128)S(1)}, u32[]{:S(2)}, u32[]{:S(2)}) collective-permute-start(f32[64,256]{1,0:T(8,128)S(1)} %add.21.mine), channel_id=1, source_target_pairs={{0,8},{2,10},{4,12},{6,14},{8,0},{10,2},{12,4},{14,6},{1,9},{3,11}... | collective-permute-start | bytes 196616 | tf_op jit(solution)/shard_map/ppermute | solution.py:45
  25.1 0.3 collective-permute-start.5
  25.4 2.5 %collective-permute-done.8.other = f32[64,256]{1,0:T(8,128)S(1)} collective-permute-done((f32[64,256]{1,0:T(8,128)S(1)}, f32[64,256]{1,0:T(8,128)S(1)}, u32[]{:S(2)}, u32[]{:S(2)}) %collective-permute-start.8) | collective-permute-done | bytes 65568 | tf_op jit(solution)/shard_map/ppermute | solution.py:45
  27.9 0.2 last_coef.1.own
  28.2 1.2 %collective-permute-done.5.across = f32[64,256]{1,0:T(8,128)S(1)} collective-permute-done((f32[64,256]{1,0:T(8,128)S(1)}, f32[64,256]{1,0:T(8,128)S(1)}, u32[]{:S(2)}, u32[]{:S(2)}) %collective-permute-start.5) | collective-permute-done | bytes 65568 | tf_op jit(solution)/shard_map/ppermute | solution.py:52
  29.4 0.5 %collective-permute-start.6 = (f32[2,64,256]{2,1,0:T(8,128)S(1)}, f32[2,64,256]{2,1,0:T(8,128)S(1)}, u32[]{:S(2)}, u32[]{:S(2)}) collective-permute-start(f32[2,64,256]{2,1,0:T(8,128)S(1)} %pad_maximum_fusion.1), channel_id=1, source_target_pairs={{0,1},{1,0},{2,3},{3,2},{4,5},{5,4},{6,7},{7,6},{8,9},{9,8},{10,11... | collective-permute-start | bytes 393224 | tf_op jit(solution)/shard_map/ppermute | solution.py:45
  29.9 2.7 %collective-permute-done.9.across = f32[64,256]{1,0:T(8,128)S(1)} collective-permute-done((f32[64,256]{1,0:T(8,128)S(1)}, f32[64,256]{1,0:T(8,128)S(1)}, u32[]{:S(2)}, u32[]{:S(2)}) %collective-permute-start.9) | collective-permute-done | bytes 65568 | tf_op jit(solution)/shard_map/ppermute | solution.py:52
  32.6 0.2 collective-permute-start.10
  32.8 0.4 %base.1 = f32[1024,256]{1,0:T(8,128)S(1)} custom-call(f32[256,1024]{1,0:T(8,128)S(1)} %get-tuple-element.23.field, f32[64,256]{1,0:T(8,128)S(1)} %get-tuple-element.28.own, f32[64,256]{1,0:T(8,128)S(1)} %collective-permute-done.5.across, f32[2,64,256]{2,1,0:T(8,128)S(1)} %collective-permute-done.6.cores, bf16[1024,256]{1,0:T(8,128)(2,1)S(1)} %get-tuple-element.21.two), custom_call_target="tpu_custom_call" | custom-call | tf_op jit(solution)/shard_map/base/pallas_call | solution.py:327
  33.1 0.3 half.1
  33.5 0.5 %collective-permute-done.10.cores = f32[2,64,256]{2,1,0:T(8,128)S(1)} collective-permute-done((f32[2,64,256]{2,1,0:T(8,128)S(1)}, f32[2,64,256]{2,1,0:T(8,128)S(1)}, u32[]{:S(2)}, u32[]{:S(2)}) %collective-permute-start.10) | collective-permute-done | bytes 131104 | tf_op jit(solution)/shard_map/ppermute | solution.py:45
  34.0 1.0 %final.1 = bf16[1024,256]{1,0:T(8,128)(2,1)} custom-call(f32[1024,256]{1,0:T(8,128)S(1)} %base.1, bf16[1024,128]{1,0:T(8,128)(2,1)S(1)} %half.1, f32[2,64,256]{2,1,0:T(8,128)S(1)} %collective-permute-done.10.cores, bf16[1024,256]{1,0:T(8,128)(2,1)S(1)} %get-tuple-element.22.three), custom_call_target="tpu_custom_call" | custom-call | tf_op jit(solution)/shard_map/final/pallas_call | solution.py:356
  (16 shorter events, 0.4 us)
Async XLA Ops:
  2.7 1.5 %collective-permute-start.2 = (f32[128,256]{1,0:T(8,128)S(1)}, f32[128,256]{1,0:T(8,128)S(1)}, u32[]{:S(2)}, u32[]{:S(2)}) collective-permute-start(f32[128,256]{1,0:T(8,128)S(1)} %get-tuple-element.27), channel_id=1, source_target_pairs={{0,1},{1,0},{2,3},{3,2},{4,5},{5,4},{6,7},{7,6},{8,9},{9,8},{10,11... | collective-permute-start | bytes 393224 | tf_op jit(solution)/shard_map/ppermute | solution.py:45
  4.1 7.5 %collective-permute-start = (f32[2,2,64,256]{3,2,1,0:T(8,128)S(1)}, f32[2,2,64,256]{3,2,1,0:T(8,128)S(1)}, u32[]{:S(2)}, u32[]{:S(2)}) collective-permute-start(f32[2,2,64,256]{3,2,1,0:T(8,128)S(1)} %get-tuple-element.25), channel_id=1, source_target_pairs={{0,1},{1,0},{2,3},{3,2},{4,5},{5,4},{6,7},{7,6},{8,9},{9,8},{10,11... | collective-permute-start | bytes 786440 | tf_op jit(solution)/shard_map/ppermute | solution.py:45
  4.3 6.2 %collective-permute-start.3 = (f32[128,256]{1,0:T(8,128)S(1)}, f32[128,256]{1,0:T(8,128)S(1)}, u32[]{:S(2)}, u32[]{:S(2)}) collective-permute-start(f32[128,256]{1,0:T(8,128)S(1)} %add.20.gram_own), channel_id=1, source_target_pairs={{0,3},{1,2},{2,1},{3,0},{4,7},{5,6},{6,5},{7,4},{8,11},{9,10},{10,... | collective-permute-start | bytes 393224 | tf_op jit(solution)/shard_map/ppermute | solution.py:52
  11.3 6.2 %collective-permute-start.4 = (f32[2,128,256]{2,1,0:T(8,128)}, f32[2,128,256]{2,1,0:T(8,128)S(1)}, u32[]{:S(2)}, u32[]{:S(2)}) collective-permute-start(f32[2,128,256]{2,1,0:T(8,128)} %pad_maximum_fusion), channel_id=1, source_target_pairs={{0,1},{1,0},{2,3},{3,2},{4,5},{5,4},{6,7},{7,6},{8,9},{9,8},{10,11... | collective-permute-start | bytes 786440 | tf_op jit(solution)/shard_map/ppermute | solution.py:45
  11.6 5.9 %copy-start = (bf16[512,512]{1,0:T(8,128)(2,1)S(1)}, bf16[512,512]{1,0:T(8,128)(2,1)}, u32[]{:S(2)}) copy-start(bf16[512,512]{1,0:T(8,128)(2,1)} %cap.2) | copy-start | bytes 1572868
  11.6 5.8 %collective-permute-start.1 = (f32[2,64,256]{2,1,0:T(8,128)S(1)}, f32[2,64,256]{2,1,0:T(8,128)S(1)}, u32[]{:S(2)}, u32[]{:S(2)}) collective-permute-start(f32[2,64,256]{2,1,0:T(8,128)S(1)} %get-tuple-element.31), channel_id=1, source_target_pairs={{0,3},{1,2},{2,1},{3,0},{4,7},{5,6},{6,5},{7,4},{8,11},{9,10},{10,... | collective-permute-start | bytes 393224 | tf_op jit(solution)/shard_map/ppermute | solution.py:52
  17.5 10.5 %copy-start.1 = (bf16[512,512]{1,0:T(8,128)(2,1)S(1)}, bf16[512,512]{1,0:T(8,128)(2,1)}, u32[]{:S(2)}) copy-start(bf16[512,512]{1,0:T(8,128)(2,1)} %cap.3) | copy-start | bytes 1572868
  18.0 4.3 %collective-permute-start.7 = (f32[64,256]{1,0:T(8,128)S(1)}, f32[64,256]{1,0:T(8,128)S(1)}, u32[]{:S(2)}, u32[]{:S(2)}) collective-permute-start(f32[64,256]{1,0:T(8,128)S(1)} %get-tuple-element.30), channel_id=1, source_target_pairs={{0,4},{2,6},{4,0},{6,2},{8,12},{10,14},{12,8},{14,10},{1,5},{3,7},... | collective-permute-start | bytes 196616 | tf_op jit(solution)/shard_map/ppermute | solution.py:45
  22.3 5.6 %collective-permute-start.8 = (f32[64,256]{1,0:T(8,128)S(1)}, f32[64,256]{1,0:T(8,128)S(1)}, u32[]{:S(2)}, u32[]{:S(2)}) collective-permute-start(f32[64,256]{1,0:T(8,128)S(1)} %add.21.mine), channel_id=1, source_target_pairs={{0,8},{2,10},{4,12},{6,14},{8,0},{10,2},{12,4},{14,6},{1,9},{3,11}... | collective-permute-start | bytes 196616 | tf_op jit(solution)/shard_map/ppermute | solution.py:45
  25.1 4.3 %collective-permute-start.5 = (f32[64,256]{1,0:T(8,128)S(1)}, f32[64,256]{1,0:T(8,128)S(1)}, u32[]{:S(2)}, u32[]{:S(2)}) collective-permute-start(f32[64,256]{1,0:T(8,128)S(1)} %get-tuple-element.29), channel_id=1, source_target_pairs={{0,3},{1,2},{2,1},{3,0},{4,7},{5,6},{6,5},{7,4},{8,11},{9,10},{10,... | collective-permute-start | bytes 196616 | tf_op jit(solution)/shard_map/ppermute | solution.py:52
  28.2 4.4 %collective-permute-start.9 = (f32[64,256]{1,0:T(8,128)S(1)}, f32[64,256]{1,0:T(8,128)S(1)}, u32[]{:S(2)}, u32[]{:S(2)}) collective-permute-start(f32[64,256]{1,0:T(8,128)S(1)} %last_coef.1.own), channel_id=1, source_target_pairs={{0,3},{1,2},{2,1},{3,0},{4,7},{5,6},{6,5},{7,4},{8,11},{9,10},{10,... | collective-permute-start | bytes 196616 | tf_op jit(solution)/shard_map/ppermute | solution.py:52
  29.4 3.3 %collective-permute-start.6 = (f32[2,64,256]{2,1,0:T(8,128)S(1)}, f32[2,64,256]{2,1,0:T(8,128)S(1)}, u32[]{:S(2)}, u32[]{:S(2)}) collective-permute-start(f32[2,64,256]{2,1,0:T(8,128)S(1)} %pad_maximum_fusion.1), channel_id=1, source_target_pairs={{0,1},{1,0},{2,3},{3,2},{4,5},{5,4},{6,7},{7,6},{8,9},{9,8},{10,11... | collective-permute-start | bytes 393224 | tf_op jit(solution)/shard_map/ppermute | solution.py:45
  32.6 1.4 %collective-permute-start.10 = (f32[2,64,256]{2,1,0:T(8,128)S(1)}, f32[2,64,256]{2,1,0:T(8,128)S(1)}, u32[]{:S(2)}, u32[]{:S(2)}) collective-permute-start(f32[2,64,256]{2,1,0:T(8,128)S(1)} %pad_maximum_fusion.2), channel_id=1, source_target_pairs={{0,1},{1,0},{2,3},{3,2},{4,5},{5,4},{6,7},{7,6},{8,9},{9,8},{10,11... | collective-permute-start | bytes 393224 | tf_op jit(solution)/shard_map/ppermute | solution.py:45

commit v7 on v6

--- a/solution.py
+++ b/solution.py
@@ -93,9 +93,10 @@
         part = field[:, i * leaf : (i + 1) * leaf].astype(BF16)
         return nn(part, one[pl.ds(i * leaf, leaf), :])
 
-    for copy in copies[:2]:
-        copy.wait()
-    solve(0)
+    copies[0].wait()
+    first = jnp.transpose(rhs[pl.ds(0, leaf), :])
+    copies[1].wait()
+    field[:, :leaf] = nt(first, inv[pl.ds(0, leaf), :])
     for copy in copies[2 : 2 * leaves + 1]:
         copy.wait()
     for i in range(1, leaves):

time: 35.2 us -> 35.2 us (level)
  no operation moved by 1% of the time
where the time goes in v7:
time: 35.2 us; the launch traced here: 35 us
  waiting for transfers between devices  17 us (48%)
  starting transfers between devices  11.1 us (32%)
  Pallas kernels  5.94 us (17%)
  other arithmetic  0.8 us (2%)
    ppermute x4, waiting for transfers between devices, across_chips(): lax.ppermute(array, ('row', 'sub'), [(i, i ^ mask) for i in range(count)])  11.2 us
    ppermute x7, starting transfers between devices, partner(): lax.ppermute(array, axis, [(i, i ^ 1 << bit) for i in range(lax.axis_size...  5.99 us
    ppermute x7, waiting for transfers between devices, partner(): lax.ppermute(array, axis, [(i, i ^ 1 << bit) for i in range(lax.axis_size...  5.85 us
    ppermute x4, starting transfers between devices, across_chips(): lax.ppermute(array, ('row', 'sub'), [(i, i ^ mask) for i in range(count)])  5.14 us
    pallas_call x1, Pallas kernels, per_device(): pl.pallas_call(functools.partial(load_kernel, leaf, bit_two), out_shape=[...  2.72 us
    pallas_call x1, Pallas kernels, per_device(): pl.pallas_call(functools.partial(final_kernel, bit_two), out_shape=jax.Sh...  1.03 us
    pallas_call x1, Pallas kernels, per_device(): pl.pallas_call(functools.partial(local_kernel, leaf, bit_two), out_shape=...  0.79 us
    another operation x3, other arithmetic, share(): return partner(jnp.stack([own, across]), 'sub', 0)  0.74 us
  transfers between devices with their start and end apart: 11, of which 8 were waited for; matrix products, arithmetic and copies ran while one was open for 2% of the time, Pallas kernels for 5%

profile of v7, /device:TPU:0, one launch (start us, length us, event | category | flops | bytes accessed | tf_op | source)
XLA Modules:
  0.0 35.0 jit_solution(12761234726732057317)
XLA Ops:
  0.0 2.7 %load.1 = (f32[128,256]{1,0:T(8,128)S(1)}, f32[128,256]{1,0:T(8,128)S(1)}, f32[256,1024]{1,0:T(8,128)S(1)}, bf16[256,512]{1,0:T(8,128)(2,1)S(1)}, bf16[1024,256]...) custom-call(bf16[1024,256]{1,0:T(8,128)(2,1)} %rhs_hbm.1, ...), custom_call_target="tpu_custom_call" | custom-call | tf_op jit(solution)/shard_map/load/pallas_call | solution.py:259
  2.7 0.6 %collective-permute-start.2 = (f32[128,256]{1,0:T(8,128)S(1)}, f32[128,256]{1,0:T(8,128)S(1)}, u32[]{:S(2)}, u32[]{:S(2)}) collective-permute-start(f32[128,256]{1,0:T(8,128)S(1)} %get-tuple-element.27), channel_id=1, source_target_pairs={{0,1},{1,0},{2,3},{3,2},{4,5},{5,4},{6,7},{7,6},{8,9},{9,8},{10,11... | collective-permute-start | bytes 393224 | tf_op jit(solution)/shard_map/ppermute | solution.py:45
  3.3 0.8 %local.1 = (f32[256,1024]{1,0:T(8,128)S(1)}, f32[2,2,64,256]{3,2,1,0:T(8,128)S(1)}, f32[2,2,64,256]{3,2,1,0:T(8,128)S(1)}) custom-call(f32[256,1024]{1,0:T(8,128)S(1)} %get-tuple-element.18.field, bf16[256,512]{1,0:T(8,128)(2,1)S(1)} %get-tuple-element.19.coef, bf16[1024,256]{1,0:T(8,128)(2,1)S(1)} %get-tuple-element.20.one, ...), custom_call_target="tpu_custom_call" | custom-call | tf_op jit(solution)/shard_map/local/pallas_call | solution.py:287
  4.3 2.7 %collective-permute-start.3 = (f32[128,256]{1,0:T(8,128)S(1)}, f32[128,256]{1,0:T(8,128)S(1)}, u32[]{:S(2)}, u32[]{:S(2)}) collective-permute-start(f32[128,256]{1,0:T(8,128)S(1)} %add.20.gram_own), channel_id=1, source_target_pairs={{0,3},{1,2},{2,1},{3,0},{4,7},{5,6},{6,5},{7,4},{8,11},{9,10},{10,... | collective-permute-start | bytes 393224 | tf_op jit(solution)/shard_map/ppermute | solution.py:52
  6.9 3.6 %collective-permute-done.3.gram_far = f32[128,256]{1,0:T(8,128)S(1)} collective-permute-done((f32[128,256]{1,0:T(8,128)S(1)}, f32[128,256]{1,0:T(8,128)S(1)}, u32[]{:S(2)}, u32[]{:S(2)}) %collective-permute-start.3) | collective-permute-done | bytes 131104 | tf_op jit(solution)/shard_map/ppermute | solution.py:52
  10.5 0.7 %pad_maximum_fusion = f32[2,128,256]{2,1,0:T(8,128)} fusion(f32[1,128,256]{2,1,0:T(8,128)S(1)} %bitcast.12, f32[1,128,256]{2,1,0:T(8,128)S(1)} %bitcast.10), kind=kLoop, calls=%fused_computation | loop fusion | flops 65536 | bytes 524288 | tf_op jit(solution)/shard_map/stack | solution.py:235
  11.3 0.3 collective-permute-start.4
  11.6 2.1 %collective-permute-start.1 = (f32[2,64,256]{2,1,0:T(8,128)S(1)}, f32[2,64,256]{2,1,0:T(8,128)S(1)}, u32[]{:S(2)}, u32[]{:S(2)}) collective-permute-start(f32[2,64,256]{2,1,0:T(8,128)S(1)} %get-tuple-element.31), channel_id=1, source_target_pairs={{0,3},{1,2},{2,1},{3,0},{4,7},{5,6},{6,5},{7,4},{8,11},{9,10},{10,... | collective-permute-start | bytes 393224 | tf_op jit(solution)/shard_map/ppermute | solution.py:52
  13.7 3.8 %collective-permute-done.1.other = f32[2,64,256]{2,1,0:T(8,128)S(1)} collective-permute-done((f32[2,64,256]{2,1,0:T(8,128)S(1)}, f32[2,64,256]{2,1,0:T(8,128)S(1)}, u32[]{:S(2)}, u32[]{:S(2)}) %collective-permute-start.1) | collective-permute-done | bytes 131104 | tf_op jit(solution)/shard_map/ppermute | solution.py:52
  17.5 0.5 %middle.1 = (f32[64,256]{1,0:T(8,128)S(1)}, f32[64,256]{1,0:T(8,128)S(1)}, f32[64,256]{1,0:T(8,128)S(1)}) custom-call(f32[2,64,256]{2,1,0:T(8,128)S(1)} %get-tuple-element.32.mine, f32[2,64,256]{2,1,0:T(8,128)S(1)} %collective-permute-done.1.other, bf16[512,512]{1,0:T(8,128)(2,1)S(1)} %copy-done, f32[128,256]{1,0:T(8,128)S(1)} %add.20.gram_own, ...), custom_call_target="tpu_custom_call" | custom-call | tf_op jit(solution)/shard_map/middle/pallas_call | solution.py:312
  18.0 1.6 %collective-permute-start.7 = (f32[64,256]{1,0:T(8,128)S(1)}, f32[64,256]{1,0:T(8,128)S(1)}, u32[]{:S(2)}, u32[]{:S(2)}) collective-permute-start(f32[64,256]{1,0:T(8,128)S(1)} %get-tuple-element.30), channel_id=1, source_target_pairs={{0,4},{2,6},{4,0},{6,2},{8,12},{10,14},{12,8},{14,10},{1,5},{3,7},... | collective-permute-start | bytes 196616 | tf_op jit(solution)/shard_map/ppermute | solution.py:45
  19.6 2.7 %collective-permute-done.7 = f32[64,256]{1,0:T(8,128)S(1)} collective-permute-done((f32[64,256]{1,0:T(8,128)S(1)}, f32[64,256]{1,0:T(8,128)S(1)}, u32[]{:S(2)}, u32[]{:S(2)}) %collective-permute-start.7) | collective-permute-done | bytes 65568 | tf_op jit(solution)/shard_map/ppermute | solution.py:45
  22.3 2.8 %collective-permute-start.8 = (f32[64,256]{1,0:T(8,128)S(1)}, f32[64,256]{1,0:T(8,128)S(1)}, u32[]{:S(2)}, u32[]{:S(2)}) collective-permute-start(f32[64,256]{1,0:T(8,128)S(1)} %add.21.mine), channel_id=1, source_target_pairs={{0,8},{2,10},{4,12},{6,14},{8,0},{10,2},{12,4},{14,6},{1,9},{3,11}... | collective-permute-start | bytes 196616 | tf_op jit(solution)/shard_map/ppermute | solution.py:45
  25.1 0.3 collective-permute-start.5
  25.4 2.5 %collective-permute-done.8.other = f32[64,256]{1,0:T(8,128)S(1)} collective-permute-done((f32[64,256]{1,0:T(8,128)S(1)}, f32[64,256]{1,0:T(8,128)S(1)}, u32[]{:S(2)}, u32[]{:S(2)}) %collective-permute-start.8) | collective-permute-done | bytes 65568 | tf_op jit(solution)/shard_map/ppermute | solution.py:45
  27.9 0.2 last_coef.1.own
  28.2 1.2 %collective-permute-done.5.across = f32[64,256]{1,0:T(8,128)S(1)} collective-permute-done((f32[64,256]{1,0:T(8,128)S(1)}, f32[64,256]{1,0:T(8,128)S(1)}, u32[]{:S(2)}, u32[]{:S(2)}) %collective-permute-start.5) | collective-permute-done | bytes 65568 | tf_op jit(solution)/shard_map/ppermute | solution.py:52
  29.4 0.5 %collective-permute-start.6 = (f32[2,64,256]{2,1,0:T(8,128)S(1)}, f32[2,64,256]{2,1,0:T(8,128)S(1)}, u32[]{:S(2)}, u32[]{:S(2)}) collective-permute-start(f32[2,64,256]{2,1,0:T(8,128)S(1)} %pad_maximum_fusion.1), channel_id=1, source_target_pairs={{0,1},{1,0},{2,3},{3,2},{4,5},{5,4},{6,7},{7,6},{8,9},{9,8},{10,11... | collective-permute-start | bytes 393224 | tf_op jit(solution)/shard_map/ppermute | solution.py:45
  29.9 2.7 %collective-permute-done.9.across = f32[64,256]{1,0:T(8,128)S(1)} collective-permute-done((f32[64,256]{1,0:T(8,128)S(1)}, f32[64,256]{1,0:T(8,128)S(1)}, u32[]{:S(2)}, u32[]{:S(2)}) %collective-permute-start.9) | collective-permute-done | bytes 65568 | tf_op jit(solution)/shard_map/ppermute | solution.py:52
  32.6 0.2 collective-permute-start.10
  32.8 0.4 %base.1 = f32[1024,256]{1,0:T(8,128)S(1)} custom-call(f32[256,1024]{1,0:T(8,128)S(1)} %get-tuple-element.23.field, f32[64,256]{1,0:T(8,128)S(1)} %get-tuple-element.28.own, f32[64,256]{1,0:T(8,128)S(1)} %collective-permute-done.5.across, f32[2,64,256]{2,1,0:T(8,128)S(1)} %collective-permute-done.6.cores, bf16[1024,256]{1,0:T(8,128)(2,1)S(1)} %get-tuple-element.21.two), custom_call_target="tpu_custom_call" | custom-call | tf_op jit(solution)/shard_map/base/pallas_call | solution.py:328
  33.1 0.3 half.1
  33.5 0.5 %collective-permute-done.10.cores = f32[2,64,256]{2,1,0:T(8,128)S(1)} collective-permute-done((f32[2,64,256]{2,1,0:T(8,128)S(1)}, f32[2,64,256]{2,1,0:T(8,128)S(1)}, u32[]{:S(2)}, u32[]{:S(2)}) %collective-permute-start.10) | collective-permute-done | bytes 131104 | tf_op jit(solution)/shard_map/ppermute | solution.py:45
  34.0 1.0 %final.1 = bf16[1024,256]{1,0:T(8,128)(2,1)} custom-call(f32[1024,256]{1,0:T(8,128)S(1)} %base.1, bf16[1024,128]{1,0:T(8,128)(2,1)S(1)} %half.1, f32[2,64,256]{2,1,0:T(8,128)S(1)} %collective-permute-done.10.cores, bf16[1024,256]{1,0:T(8,128)(2,1)S(1)} %get-tuple-element.22.three), custom_call_target="tpu_custom_call" | custom-call | tf_op jit(solution)/shard_map/final/pallas_call | solution.py:357
  (16 shorter events, 0.4 us)
Async XLA Ops:
  2.7 1.5 %collective-permute-start.2 = (f32[128,256]{1,0:T(8,128)S(1)}, f32[128,256]{1,0:T(8,128)S(1)}, u32[]{:S(2)}, u32[]{:S(2)}) collective-permute-start(f32[128,256]{1,0:T(8,128)S(1)} %get-tuple-element.27), channel_id=1, source_target_pairs={{0,1},{1,0},{2,3},{3,2},{4,5},{5,4},{6,7},{7,6},{8,9},{9,8},{10,11... | collective-permute-start | bytes 393224 | tf_op jit(solution)/shard_map/ppermute | solution.py:45
  4.1 7.5 %collective-permute-start = (f32[2,2,64,256]{3,2,1,0:T(8,128)S(1)}, f32[2,2,64,256]{3,2,1,0:T(8,128)S(1)}, u32[]{:S(2)}, u32[]{:S(2)}) collective-permute-start(f32[2,2,64,256]{3,2,1,0:T(8,128)S(1)} %get-tuple-element.25), channel_id=1, source_target_pairs={{0,1},{1,0},{2,3},{3,2},{4,5},{5,4},{6,7},{7,6},{8,9},{9,8},{10,11... | collective-permute-start | bytes 786440 | tf_op jit(solution)/shard_map/ppermute | solution.py:45
  4.3 6.2 %collective-permute-start.3 = (f32[128,256]{1,0:T(8,128)S(1)}, f32[128,256]{1,0:T(8,128)S(1)}, u32[]{:S(2)}, u32[]{:S(2)}) collective-permute-start(f32[128,256]{1,0:T(8,128)S(1)} %add.20.gram_own), channel_id=1, source_target_pairs={{0,3},{1,2},{2,1},{3,0},{4,7},{5,6},{6,5},{7,4},{8,11},{9,10},{10,... | collective-permute-start | bytes 393224 | tf_op jit(solution)/shard_map/ppermute | solution.py:52
  11.3 6.2 %collective-permute-start.4 = (f32[2,128,256]{2,1,0:T(8,128)}, f32[2,128,256]{2,1,0:T(8,128)S(1)}, u32[]{:S(2)}, u32[]{:S(2)}) collective-permute-start(f32[2,128,256]{2,1,0:T(8,128)} %pad_maximum_fusion), channel_id=1, source_target_pairs={{0,1},{1,0},{2,3},{3,2},{4,5},{5,4},{6,7},{7,6},{8,9},{9,8},{10,11... | collective-permute-start | bytes 786440 | tf_op jit(solution)/shard_map/ppermute | solution.py:45
  11.6 5.9 %copy-start = (bf16[512,512]{1,0:T(8,128)(2,1)S(1)}, bf16[512,512]{1,0:T(8,128)(2,1)}, u32[]{:S(2)}) copy-start(bf16[512,512]{1,0:T(8,128)(2,1)} %cap.2) | copy-start | bytes 1572868
  11.6 5.8 %collective-permute-start.1 = (f32[2,64,256]{2,1,0:T(8,128)S(1)}, f32[2,64,256]{2,1,0:T(8,128)S(1)}, u32[]{:S(2)}, u32[]{:S(2)}) collective-permute-start(f32[2,64,256]{2,1,0:T(8,128)S(1)} %get-tuple-element.31), channel_id=1, source_target_pairs={{0,3},{1,2},{2,1},{3,0},{4,7},{5,6},{6,5},{7,4},{8,11},{9,10},{10,... | collective-permute-start | bytes 393224 | tf_op jit(solution)/shard_map/ppermute | solution.py:52
  17.5 10.5 %copy-start.1 = (bf16[512,512]{1,0:T(8,128)(2,1)S(1)}, bf16[512,512]{1,0:T(8,128)(2,1)}, u32[]{:S(2)}) copy-start(bf16[512,512]{1,0:T(8,128)(2,1)} %cap.3) | copy-start | bytes 1572868
  18.0 4.3 %collective-permute-start.7 = (f32[64,256]{1,0:T(8,128)S(1)}, f32[64,256]{1,0:T(8,128)S(1)}, u32[]{:S(2)}, u32[]{:S(2)}) collective-permute-start(f32[64,256]{1,0:T(8,128)S(1)} %get-tuple-element.30), channel_id=1, source_target_pairs={{0,4},{2,6},{4,0},{6,2},{8,12},{10,14},{12,8},{14,10},{1,5},{3,7},... | collective-permute-start | bytes 196616 | tf_op jit(solution)/shard_map/ppermute | solution.py:45
  22.3 5.6 %collective-permute-start.8 = (f32[64,256]{1,0:T(8,128)S(1)}, f32[64,256]{1,0:T(8,128)S(1)}, u32[]{:S(2)}, u32[]{:S(2)}) collective-permute-start(f32[64,256]{1,0:T(8,128)S(1)} %add.21.mine), channel_id=1, source_target_pairs={{0,8},{2,10},{4,12},{6,14},{8,0},{10,2},{12,4},{14,6},{1,9},{3,11}... | collective-permute-start | bytes 196616 | tf_op jit(solution)/shard_map/ppermute | solution.py:45
  25.1 4.3 %collective-permute-start.5 = (f32[64,256]{1,0:T(8,128)S(1)}, f32[64,256]{1,0:T(8,128)S(1)}, u32[]{:S(2)}, u32[]{:S(2)}) collective-permute-start(f32[64,256]{1,0:T(8,128)S(1)} %get-tuple-element.29), channel_id=1, source_target_pairs={{0,3},{1,2},{2,1},{3,0},{4,7},{5,6},{6,5},{7,4},{8,11},{9,10},{10,... | collective-permute-start | bytes 196616 | tf_op jit(solution)/shard_map/ppermute | solution.py:52
  28.2 4.4 %collective-permute-start.9 = (f32[64,256]{1,0:T(8,128)S(1)}, f32[64,256]{1,0:T(8,128)S(1)}, u32[]{:S(2)}, u32[]{:S(2)}) collective-permute-start(f32[64,256]{1,0:T(8,128)S(1)} %last_coef.1.own), channel_id=1, source_target_pairs={{0,3},{1,2},{2,1},{3,0},{4,7},{5,6},{6,5},{7,4},{8,11},{9,10},{10,... | collective-permute-start | bytes 196616 | tf_op jit(solution)/shard_map/ppermute | solution.py:52
  29.4 3.3 %collective-permute-start.6 = (f32[2,64,256]{2,1,0:T(8,128)S(1)}, f32[2,64,256]{2,1,0:T(8,128)S(1)}, u32[]{:S(2)}, u32[]{:S(2)}) collective-permute-start(f32[2,64,256]{2,1,0:T(8,128)S(1)} %pad_maximum_fusion.1), channel_id=1, source_target_pairs={{0,1},{1,0},{2,3},{3,2},{4,5},{5,4},{6,7},{7,6},{8,9},{9,8},{10,11... | collective-permute-start | bytes 393224 | tf_op jit(solution)/shard_map/ppermute | solution.py:45
  32.6 1.4 %collective-permute-start.10 = (f32[2,64,256]{2,1,0:T(8,128)S(1)}, f32[2,64,256]{2,1,0:T(8,128)S(1)}, u32[]{:S(2)}, u32[]{:S(2)}) collective-permute-start(f32[2,64,256]{2,1,0:T(8,128)S(1)} %pad_maximum_fusion.2), channel_id=1, source_target_pairs={{0,1},{1,0},{2,3},{3,2},{4,5},{5,4},{6,7},{7,6},{8,9},{9,8},{10,11... | collective-permute-start | bytes 393224 | tf_op jit(solution)/shard_map/ppermute | solution.py:45
